TPU v7x, 256 devices: a whole 4x4x8 slice. The times are simulated.
256 devices in a mesh: grp: 2 (over core), tok: 32 (over z, y), head: 4 (over x).
Axes of the slice: x: 4, y: 4, z: 8, core: 2. Of those that a mesh axis runs over, the one named last changes fastest.
Arguments:
- hidden_in: bfloat16 [2, 4096, 2560], P('grp', 'tok', 'head'), may hold values from -6 to 6
- attn_gain: bfloat16 [2560], replicated, may hold values from 0.5 to 1.5
- w_query: bfloat16 [2560, 2560], P('grp', 'head'), may hold values from -0.125 to 0.125
- key_projection_weight: bfloat16 [2560, 512], P('grp', 'head'), may hold values from -0.25 to 0.25
- value_projection_weight: bfloat16 [2560, 512], P('grp', 'head'), may hold values from -0.125 to 0.125
- w_out: bfloat16 [2560, 2560], P('grp', 'head'), may hold values from -0.125 to 0.125
- prefix_keys: bfloat16 [2, 2048, 4, 128], P('grp', 'tok', 'head'), may hold values from -91 to 91
- cached_prefix_values: bfloat16 [2, 2048, 4, 128], P('grp', 'tok', 'head'), may hold values from -6 to 6
- request_lengths: int32 [2, 16], P('grp'), may hold values from 1 to 1024, 4096 in all within a row
- moe_gain: bfloat16 [2560], replicated, may hold values from 0.5 to 1.5
- expert_ids: int32 [2, 4096, 6], P('grp', 'tok'), may hold values from 0 to 63, all different within a row; in each aligned block of 128 rows (0 to 127, 128 to 255, ..., all dimensions but the last counted through in order) at most 16 rows name the same one
- route_weights: float32 [2, 4096, 6], P('grp', 'tok'), may hold values from 0.05 to 0.3
- w_gate: bfloat16 [64, 2560, 1536], P(('grp', 'tok'), None, 'head'), may hold values from -0.125 to 0.125
- w_up: bfloat16 [64, 2560, 1536], P(('grp', 'tok'), None, 'head'), may hold values from -0.125 to 0.125
- w_down: bfloat16 [64, 1536, 2560], P(('grp', 'tok'), None, 'head'), may hold values from -0.15625 to 0.15625
Outputs:
- hidden_out: bfloat16 [2, 4096, 2560], P('grp', 'tok', 'head')
Inputs may be any that keep to these rules, and one draw needn't show every extreme that they name: `expert_ids`: each token names 6 different experts. Among the tokens of one device (aligned blocks of 128 tokens of a group) no expert is named more than 16 times.
All inputs are finite; a program needn't handle non-finite values.
Results may differ from a plain program's by a relative error of at most 0.011.
Values may be sent and summed in bfloat16 or wider, within the bound.
A program may use at most 64 MiB of HBM per device.

v0:
```python
import math

import jax
import jax.numpy as jnp
from jax import lax
from jax.sharding import PartitionSpec as P

ROPE_BASE = 500000.0
NORM_EPS = 1e-06
MASKED = -1e30


def shifted(block, axis, distance):
    devices = range(lax.axis_size(axis))
    route = [(i - distance, i) for i in devices if i - distance in devices]
    return lax.ppermute(block, axis, route)


def rms_norm(values_in, gain_vector):
    widened = values_in.astype(jnp.float32)
    mean_sq = jnp.mean(widened * widened, axis=-1, keepdims=True)
    return (widened * lax.rsqrt(mean_sq + NORM_EPS) * gain_vector.astype(jnp.float32)).astype(
        jnp.bfloat16
    )


def apply_rotary(product, token_positions):
    half_dim = product.shape[-1] // 2
    frequency = jnp.exp(
        jnp.arange(half_dim, dtype=jnp.float32) * (-2.0 * math.log(ROPE_BASE) / product.shape[-1])
    )
    angles = token_positions.astype(jnp.float32)[:, None] * frequency[None, :]
    cosine = jnp.cos(angles)[:, None, :]
    sine_part = jnp.sin(angles)[:, None, :]
    first_half = product[..., :half_dim]
    second_half = product[..., half_dim:]
    turned = jnp.concatenate(
        [
            first_half * cosine - second_half * sine_part,
            second_half * cosine + first_half * sine_part,
        ],
        axis=-1,
    )
    return turned.astype(jnp.bfloat16)


def attend(running, queries, keys_block, values_block, visible):
    row_max, row_total, summed = running
    scores = jnp.einsum(
        "tcrd,kcd->ctrk", queries, keys_block, preferred_element_type=jnp.float32
    ) * queries.shape[-1] ** (-0.5)
    if visible is not None:
        scores = jnp.where(visible[None, :, None, :], scores, MASKED)
    new_max = jnp.maximum(row_max, jnp.max(scores, axis=-1))
    weights = jnp.exp(scores - new_max[..., None])
    if visible is not None:
        weights = jnp.where(visible[None, :, None, :], weights, 0.0)
    factor = jnp.exp(row_max - new_max)
    row_total = row_total * factor + jnp.sum(weights, axis=-1)
    summed = summed * factor[..., None] + jnp.einsum(
        "ctrk,kcd->ctrd",
        weights.astype(jnp.bfloat16),
        values_block,
        preferred_element_type=jnp.float32,
    )
    return (new_max, row_total, summed)


def on_device(
    hidden_in,
    attn_gain,
    w_query,
    key_projection_weight,
    value_projection_weight,
    w_out,
    prefix_keys,
    cached_prefix_values,
    request_lengths,
    moe_gain,
    expert_ids,
    route_weights,
    w_gate,
    w_up,
    w_down,
):
    tok_count = lax.axis_size("tok")
    grp_count = lax.axis_size("grp")
    tok_rank = lax.axis_index("tok")
    head_rank = lax.axis_index("head")
    tok_dev = hidden_in.shape[1]
    model_width = attn_gain.shape[0]
    head_dim = prefix_keys.shape[3]
    kv_local = prefix_keys.shape[2]
    group_length = w_query.shape[1] // (kv_local * head_dim)
    prefix_total = prefix_keys.shape[1] * tok_count
    quarter = hidden_in[0]
    features = lax.all_gather(quarter, "head", axis=1, tiled=True)
    attention_input = rms_norm(features, attn_gain)
    lengths = request_lengths[0]
    request_ends = jnp.cumsum(lengths)
    starts = request_ends - lengths
    token_index = tok_rank * tok_dev + jnp.arange(tok_dev, dtype=jnp.int32)
    own_start = jnp.max(
        jnp.where(starts[None, :] <= token_index[:, None], starts[None, :], 0), axis=1
    )
    token_positions = prefix_total + token_index - own_start
    full_query, full_key, full_value, full_out = (
        lax.all_gather(w_query, "grp", axis=0, tiled=True),
        lax.all_gather(key_projection_weight, "grp", axis=0, tiled=True),
        lax.all_gather(value_projection_weight, "grp", axis=0, tiled=True),
        lax.all_gather(w_out, "grp", axis=0, tiled=True),
    )
    query_product = jnp.dot(attention_input, full_query, preferred_element_type=jnp.float32)
    key_product = jnp.dot(attention_input, full_key, preferred_element_type=jnp.float32)
    value_product = jnp.dot(attention_input, full_value, preferred_element_type=jnp.float32)
    queries = apply_rotary(
        query_product.reshape(tok_dev, kv_local * group_length, head_dim), token_positions
    )
    queries = queries.reshape(tok_dev, kv_local, group_length, head_dim)
    request_suffix_keys = apply_rotary(
        key_product.reshape(tok_dev, kv_local, head_dim), token_positions
    )
    request_suffix_values = value_product.astype(jnp.bfloat16).reshape(tok_dev, kv_local, head_dim)
    running = (
        jnp.full((kv_local, tok_dev, group_length), MASKED, jnp.float32),
        jnp.zeros((kv_local, tok_dev, group_length), jnp.float32),
        jnp.zeros((kv_local, tok_dev, group_length, head_dim), jnp.float32),
    )
    running = attend(
        running,
        queries,
        lax.all_gather(prefix_keys[0], "tok", axis=0, tiled=True),
        lax.all_gather(cached_prefix_values[0], "tok", axis=0, tiled=True),
        None,
    )

    def visible_from(first_index, count):
        key_index = first_index + jnp.arange(count, dtype=jnp.int32)
        return (key_index[None, :] >= own_start[:, None]) & (
            key_index[None, :] <= token_index[:, None]
        )

    running = attend(
        running,
        queries,
        request_suffix_keys,
        request_suffix_values,
        visible_from(tok_rank * tok_dev, tok_dev),
    )
    longest = tok_dev * tok_count // 4
    reach_devices = (longest - 1 + tok_dev - 1) // tok_dev
    stacked = jnp.stack([request_suffix_keys, request_suffix_values])
    for distance in range(1, reach_devices + 1):
        arrived = shifted(stacked, "tok", distance)
        running = attend(
            running,
            queries,
            arrived[0],
            arrived[1],
            visible_from((tok_rank - distance) * tok_dev, tok_dev),
        )
    row_max, row_total, summed = running
    attended = (summed / row_total[..., None]).astype(jnp.bfloat16)
    attended = jnp.transpose(attended, (1, 0, 2, 3)).reshape(
        tok_dev, kv_local * group_length * head_dim
    )
    partial_value = lax.dot_general(
        attended, full_out, (((1,), (1,)), ((), ())), preferred_element_type=jnp.float32
    )
    share_width = model_width // lax.axis_size("head")
    mixed_sum = lax.psum(partial_value.astype(jnp.bfloat16), "head").astype(jnp.float32)
    mid_full = (features.astype(jnp.float32) + mixed_sum).astype(jnp.bfloat16)
    mid_quarter = lax.dynamic_slice_in_dim(mid_full, head_rank * share_width, share_width, 1)
    moe_in = rms_norm(mid_full, moe_gain)
    experts = grp_count * tok_count * w_gate.shape[0]
    top_count = expert_ids.shape[2]
    capacity = 4 * tok_dev * top_count // (3 * experts)
    chosen = expert_ids[0].reshape(-1)
    onehot = (chosen[:, None] == jnp.arange(experts, dtype=jnp.int32)[None, :]).astype(jnp.int32)
    slot_rank = jnp.sum(onehot * jnp.cumsum(onehot, axis=0), axis=1) - 1
    slot_place = chosen * capacity + slot_rank
    choice_token = jnp.arange(tok_dev * top_count, dtype=jnp.int32) // top_count
    source = jnp.full((experts * capacity,), tok_dev, jnp.int32).at[slot_place].set(choice_token)
    outgoing = jnp.take(moe_in, source, axis=0, mode="fill", fill_value=0).reshape(
        experts, capacity, model_width
    )
    incoming = lax.all_to_all(outgoing, ("grp", "tok"), split_axis=0, concat_axis=0, tiled=True)
    flat_rows = incoming.reshape(-1, model_width)
    gate_act = jnp.dot(flat_rows, w_gate[0], preferred_element_type=jnp.float32)
    up_act = jnp.dot(flat_rows, w_up[0], preferred_element_type=jnp.float32)
    hidden = (jax.nn.silu(gate_act) * up_act).astype(jnp.bfloat16)
    down_rows = w_down[0]
    result = jnp.dot(
        lax.all_gather(hidden, "head", axis=1, tiled=True),
        down_rows,
        preferred_element_type=jnp.float32,
    )
    expert_out = result.astype(jnp.bfloat16).reshape(
        incoming.shape[0], incoming.shape[1], w_down.shape[2]
    )
    returned = lax.all_to_all(expert_out, ("grp", "tok"), split_axis=0, concat_axis=0, tiled=True)
    returned = returned.reshape(experts * capacity, share_width)
    picked = jnp.take(returned, slot_place, axis=0).astype(jnp.float32)
    weighted = jnp.sum(
        (picked * route_weights[0].reshape(-1)[:, None]).reshape(tok_dev, top_count, share_width),
        axis=1,
    )
    output = (mid_quarter.astype(jnp.float32) + weighted).astype(jnp.bfloat16)
    return output[None]


def solution(mesh):
    return jax.shard_map(
        on_device,
        mesh=mesh,
        in_specs=(
            P("grp", "tok", "head"),
            P(),
            P("grp", "head"),
            P("grp", "head"),
            P("grp", "head"),
            P("grp", "head"),
            P("grp", "tok", "head", None),
            P("grp", "tok", "head", None),
            P("grp", None),
            P(),
            P("grp", "tok", None),
            P("grp", "tok", None),
            P(("grp", "tok"), None, "head"),
            P(("grp", "tok"), None, "head"),
            P(("grp", "tok"), None, "head"),
        ),
        out_specs=P("grp", "tok", "head"),
        check_vma=False,
    )
```

profile of v0, /device:TPU:1, one launch (start us, length us, event | category | flops | bytes accessed | tf_op | source)
XLA Modules:
  0.0 505.7 jit_solution(13813160702682913209)
XLA Ops:
  9.6 13.2 %all-gather = bf16[1,128,2560]{2,1,0:T(8,128)(2,1)S(1)} all-gather(bf16[1,128,640]{2,1,0:T(8,128)(2,1)} %param.15), channel_id=2, replica_groups=mesh['grp'=2,'tok'=32,'head'=4] {'head'}, dimensions={2}, use_global_device_ids=true | all-gather | bytes 819200 | tf_op jit(solution)/shard_map/all_gather | solution.py:97
  23.1 6.3 %all_gather.28 = bf16[2560,128]{1,0:T(8,128)(2,1)S(1)} all-gather(bf16[1280,128]{1,0:T(8,128)(2,1)S(1)} %copy-done.2), channel_id=1, replica_groups=mesh['grp'=2,'tok'=32,'head'=4] {'grp'}, dimensions={0}, use_global_device_ids=true | all-gather | bytes 983040 | tf_op jit(solution)/shard_map/all_gather | solution.py:109
  29.4 2.3 all_gather.29
  33.6 1.9 collective-permute-start
  35.5 4.6 collective-permute-start.1
  40.1 4.3 collective-permute-start.2
  44.4 3.6 collective-permute-start.3
  48.0 3.9 collective-permute-start.4
  57.8 39.5 %all-gather.1 = bf16[1,2048,1,128]{3,1,2,0:T(8,128)(2,1)S(1)} all-gather(bf16[1,64,1,128]{3,1,2,0:T(8,128)(2,1)S(1)} %copy-done.19), channel_id=3, replica_groups=mesh['grp'=2,'tok'=32,'head'=4] {'tok'}, dimensions={1}, use_global_device_ids=true | all-gather | bytes 540672 | tf_op jit(solution)/shard_map/all_gather | solution.py:132
  97.3 39.7 %all-gather.2 = bf16[1,2048,1,128]{3,1,2,0:T(8,128)(2,1)} all-gather(bf16[1,64,1,128]{3,1,2,0:T(8,128)(2,1)S(1)} %copy-done.20), channel_id=4, replica_groups=mesh['grp'=2,'tok'=32,'head'=4] {'tok'}, dimensions={1}, use_global_device_ids=true | all-gather | bytes 540672 | tf_op jit(solution)/shard_map/all_gather | solution.py:133
  137.6 1.8 reduce-window.9
  141.3 1.6 compare_and_fusion.8
  142.9 3.4 fusion.156
  147.0 1.1 copy.185
  148.1 1.8 copy.186
  149.9 1.1 subtract_convert_fusion
  152.1 3.0 collective-permute-start.5
  155.2 1.0 fusion.169
  156.2 4.6 collective-permute-start.6
  160.8 1.0 fusion.168
  161.9 3.4 collective-permute-start.7
  165.2 1.0 fusion.167
  166.3 1.0 fusion.166
  167.3 1.0 fusion.165
  170.1 1.0 fusion
  172.1 1.0 fusion.90
  173.2 1.0 fusion.88
  174.1 1.0 fusion.86
  175.8 1.2 fusion.52
  177.2 1.1 fusion.55
  178.4 4.0 convolution_convert_fusion
  182.5 3.4 scatter_custom_fusion
  186.0 66.5 %all-reduce.2.cloned.1.call-done = bf16[128,2560]{1,0:T(8,128)(2,1)} async-done(((bf16[128,2560]{1,0:T(8,128)(2,1)}), bf16[128,2560]{1,0:T(8,128)(2,1)}) %all-reduce.2.cloned.1.call-update) | async-done | bytes 655376 | tf_op jit(solution)/shard_map/psum | solution.py:171
  252.6 2.2 fusion.17
  254.8 1.3 fusion.19
  256.1 6.3 %gather_fusion = bf16[1024,2560]{1,0:T(8,128)(2,1)} fusion(bf16[128,2560]{1,0:T(8,128)(2,1)S(1)} %fusion.19, s32[1024]{0:T(1024)S(1)} %fusion.138), kind=kCustom, calls=%fused_computation | custom fusion | bytes 10489856 | tf_op jit(solution)/shard_map/jit(_take)/gather | solution.py:184
  262.4 2.9 broadcast_select_fusion
  265.3 130.5 %all_to_all.10 = bf16[64,16,2560]{2,1,0:T(8,128)(2,1)S(1)} all-to-all(bf16[64,16,2560]{2,1,0:T(8,128)(2,1)S(1)} %broadcast_select_fusion), channel_id=1, replica_groups=mesh['grp'=2,'tok'=32,'head'=4] {'grp','tok'}, dimensions={0} | all-to-all | bytes 10485760 | tf_op jit(solution)/shard_map/all_to_all | solution.py:187
  395.8 2.9 fusion.10
  398.7 3.8 multiply_convert_fusion
  402.6 38.6 %all-gather.11.cloned.1.call-done = bf16[1024,1536]{1,0:T(8,128)(2,1)} async-done(((bf16[1024,384]{1,0:T(8,128)(2,1)}), bf16[1024,1536]{1,0:T(8,128)(2,1)}) %all-gather.11.cloned.1.call-update) | async-done | bytes 3145744 | tf_op jit(solution)/shard_map/all_gather | solution.py:194
  441.2 5.6 %fusion.12 = bf16[1024,640]{1,0:T(8,128)(2,1)} fusion(bf16[1024,1536]{1,0:T(8,128)(2,1)} %all-gather.11.cloned.1.call-done, bf16[1,1536,640]{2,1,0:T(8,128)(2,1)S(1)} %copy-done), kind=kOutput, calls=%fused_computation.24 | convolution fusion | flops 2013921280 | bytes 6422528 | tf_op jit(solution)/shard_map/dot_general | solution.py:193
  446.7 10.9 %all-to-all-start.1 = ((bf16[64,16,640]{2,1,0:T(8,128)(2,1)}), bf16[64,16,640]{2,1,0:T(8,128)(2,1)S(1)}, u32[]{:S(2)}, u32[]{:S(2)}) async-start(bf16[64,16,640]{2,1,0:T(8,128)(2,1)} %bitcast.201), calls=%async_computation.1 | async-start | bytes 2621440 | tf_op jit(solution)/shard_map/all_to_all | solution.py:201
  458.2 32.9 %all-to-all-done.1 = bf16[64,16,640]{2,1,0:T(8,128)(2,1)S(1)} async-done(((bf16[64,16,640]{2,1,0:T(8,128)(2,1)}), bf16[64,16,640]{2,1,0:T(8,128)(2,1)S(1)}, u32[]{:S(2)}, u32[]{:S(2)}) %all-to-all-start.1) | async-done | bytes 1310752 | tf_op jit(solution)/shard_map/all_to_all | solution.py:201
  491.0 3.4 gather_fusion.1
  494.4 2.1 gather.15
  496.5 1.0 multiply_reduce_fusion.1
  497.5 1.6 fusion.96
  (141 shorter events, 19.6 us)
Async XLA Ops:
  6.5 434.6 %copy-start = (bf16[1,1536,640]{2,1,0:T(8,128)(2,1)S(1)}, bf16[1,1536,640]{2,1,0:T(8,128)(2,1)}, u32[]{:S(2)}) copy-start(bf16[1,1536,640]{2,1,0:T(8,128)(2,1)} %param.29) | copy-start | bytes 5898244
  6.5 16.6 %copy-start.2 = (bf16[1280,128]{1,0:T(8,128)(2,1)S(1)}, bf16[1280,128]{1,0:T(8,128)(2,1)}, u32[]{:S(2)}) copy-start(bf16[1280,128]{1,0:T(8,128)(2,1)} %param.18) | copy-start | bytes 983044
  6.5 22.8 %copy-start.3 = (bf16[1280,128]{1,0:T(8,128)(2,1)S(1)}, bf16[1280,128]{1,0:T(8,128)(2,1)}, u32[]{:S(2)}) copy-start(bf16[1280,128]{1,0:T(8,128)(2,1)} %param.19) | copy-start | bytes 983044
  6.5 136.4 %all-gather.7.cloned.1.call-start = ((), (), s32[]{:S(2)}) async-start(), calls=%async_computation.2 | async-start | bytes 4915200 | tf_op jit(solution)/shard_map/all_gather | solution.py:108
  7.3 171.2 %all-gather.9.cloned.1.call-start = ((), (), s32[]{:S(2)}) async-start(), calls=%async_computation.3 | async-start | bytes 4915200 | tf_op jit(solution)/shard_map/all_gather | solution.py:111
  8.0 24.4 %copy-start.15 = (f32[2560]{0:T(1024)}, f32[2560]{0:T(1024)S(1)}, u32[]{:S(2)}) copy-start(f32[2560]{0:T(1024)S(1)} %convert_element_type.128) | copy-start | bytes 30724
  8.9 0.7 copy-start.24
  9.6 22.5 %copy-start.25 = (s32[128]{0:T(128)}, s32[128]{0:T(128)S(1)}, u32[]{:S(2)}) copy-start(s32[128]{0:T(128)S(1)} %select_reduce_fusion) | copy-start | bytes 1540
  31.7 20.3 %copy-start.26 = (f32[128]{0:T(128)}, f32[128]{0:T(128)S(1)}, u32[]{:S(2)}) copy-start(f32[128]{0:T(128)S(1)} %add_rsqrt_fusion.1) | copy-start | bytes 1540
  32.2 20.8 %copy-start.17 = (s32[1,128,6]{1,0,2:T(1,128)S(1)}, s32[1,128,6]{1,0,2:T(1,128)}, u32[]{:S(2)}) copy-start(s32[1,128,6]{1,0,2:T(1,128)} %param.25) | copy-start | bytes 9220
  32.2 25.6 %copy-start.19 = (bf16[1,64,1,128]{3,1,2,0:T(8,128)(2,1)S(1)}, bf16[1,64,1,128]{3,1,2,0:T(8,128)(2,1)}, u32[]{:S(2)}) copy-start(bf16[1,64,1,128]{3,1,2,0:T(8,128)(2,1)} %param.21) | copy-start | bytes 49156
  32.4 0.6 copy-start.8
  32.4 1.2 copy-start.10
  32.4 64.8 %copy-start.20 = (bf16[1,64,1,128]{3,1,2,0:T(8,128)(2,1)S(1)}, bf16[1,64,1,128]{3,1,2,0:T(8,128)(2,1)}, u32[]{:S(2)}) copy-start(bf16[1,64,1,128]{3,1,2,0:T(8,128)(2,1)} %param.22) | copy-start | bytes 49156
  32.9 2.6 copy-start.12
  32.9 104.1 %copy-start.22 = (bf16[2560]{0:T(1024)(128)(2,1)S(1)}, bf16[2560]{0:T(1024)(128)(2,1)}, u32[]{:S(2)}) copy-start(bf16[2560]{0:T(1024)(128)(2,1)} %param.24) | copy-start | bytes 15364
  33.6 118.5 %collective-permute-start = (bf16[2,128,1,128]{1,3,2,0:T(8,128)(2,1)}, bf16[2,128,1,128]{1,3,2,0:T(8,128)(2,1)}, u32[]{:S(2)}, u32[]{:S(2)}) collective-permute-start(bf16[2,128,1,128]{1,3,2,0:T(8,128)(2,1)} %pad_maximum_fusion.1), channel_id=1, source_target_pairs={{0,4},{4,8},{8,12},{12,16},{16,20},{20,24},{24,28},{28,32},{32,36}... | collective-permute-start | bytes 196616 | tf_op jit(solution)/shard_map/ppermute | solution.py:16
  35.5 120.7 %collective-permute-start.1 = (bf16[2,128,1,128]{1,3,2,0:T(8,128)(2,1)}, bf16[2,128,1,128]{1,3,2,0:T(8,128)(2,1)}, u32[]{:S(2)}, u32[]{:S(2)}) collective-permute-start(bf16[2,128,1,128]{1,3,2,0:T(8,128)(2,1)} %pad_maximum_fusion.1), channel_id=1, source_target_pairs={{0,8},{4,12},{8,16},{12,20},{16,24},{20,28},{24,32},{28,36},{32,40... | collective-permute-start | bytes 196616 | tf_op jit(solution)/shard_map/ppermute | solution.py:16
  40.1 121.7 %collective-permute-start.2 = (bf16[2,128,1,128]{1,3,2,0:T(8,128)(2,1)}, bf16[2,128,1,128]{1,3,2,0:T(8,128)(2,1)}, u32[]{:S(2)}, u32[]{:S(2)}) collective-permute-start(bf16[2,128,1,128]{1,3,2,0:T(8,128)(2,1)} %pad_maximum_fusion.1), channel_id=1, source_target_pairs={{0,12},{4,16},{8,20},{12,24},{16,28},{20,32},{24,36},{28,40},{32,4... | collective-permute-start | bytes 196616 | tf_op jit(solution)/shard_map/ppermute | solution.py:16
  44.4 121.8 %collective-permute-start.3 = (bf16[2,128,1,128]{1,3,2,0:T(8,128)(2,1)}, bf16[2,128,1,128]{1,3,2,0:T(8,128)(2,1)}, u32[]{:S(2)}, u32[]{:S(2)}) collective-permute-start(bf16[2,128,1,128]{1,3,2,0:T(8,128)(2,1)} %pad_maximum_fusion.1), channel_id=1, source_target_pairs={{0,16},{4,20},{8,24},{12,28},{16,32},{20,36},{24,40},{28,44},{32,4... | collective-permute-start | bytes 196616 | tf_op jit(solution)/shard_map/ppermute | solution.py:16
  48.0 119.3 %collective-permute-start.4 = (bf16[2,128,1,128]{1,3,2,0:T(8,128)(2,1)}, bf16[2,128,1,128]{1,3,2,0:T(8,128)(2,1)}, u32[]{:S(2)}, u32[]{:S(2)}) collective-permute-start(bf16[2,128,1,128]{1,3,2,0:T(8,128)(2,1)} %pad_maximum_fusion.1), channel_id=1, source_target_pairs={{0,20},{4,24},{8,28},{12,32},{16,36},{20,40},{24,44},{28,48},{32,5... | collective-permute-start | bytes 196616 | tf_op jit(solution)/shard_map/ppermute | solution.py:16
  52.0 200.6 %all-reduce.2.cloned.1.call-start = ((), (), s32[]{:S(2)}) async-start(), calls=%async_computation.4 | async-start | bytes 1310720 | tf_op jit(solution)/shard_map/psum | solution.py:171
  151.1 9.7 %copy-start.7 = (pred[128,128]{0,1:T(8,128)(4,1)S(1)}, pred[128,128]{0,1:T(8,128)(4,1)}, u32[]{:S(2)}) copy-start(pred[128,128]{0,1:T(8,128)(4,1)} %get-tuple-element.42) | copy-start | bytes 49156
  151.2 14.1 %copy-start.6 = (pred[128,128]{0,1:T(8,128)(4,1)S(1)}, pred[128,128]{0,1:T(8,128)(4,1)}, u32[]{:S(2)}) copy-start(pred[128,128]{0,1:T(8,128)(4,1)} %get-tuple-element.35) | copy-start | bytes 49156
  151.2 15.1 %copy-start.5 = (pred[128,128]{0,1:T(8,128)(4,1)S(1)}, pred[128,128]{0,1:T(8,128)(4,1)}, u32[]{:S(2)}) copy-start(pred[128,128]{0,1:T(8,128)(4,1)} %get-tuple-element.36) | copy-start | bytes 49156
  152.1 15.2 %copy-start.4 = (pred[128,128]{0,1:T(8,128)(4,1)S(1)}, pred[128,128]{0,1:T(8,128)(4,1)}, u32[]{:S(2)}) copy-start(pred[128,128]{0,1:T(8,128)(4,1)} %get-tuple-element.37) | copy-start | bytes 49156
  152.1 16.8 %copy-start.9 = (bf16[128,1,64]{0,2,1:T(8,128)(2,1)S(1)}, bf16[128,1,64]{0,2,1:T(8,128)(2,1)}, u32[]{:S(2)}) copy-start(bf16[128,1,64]{0,2,1:T(8,128)(2,1)} %copy-done.8) | copy-start | bytes 49156
  152.1 16.8 %copy-start.11 = (bf16[128,1,64]{0,2,1:T(8,128)(2,1)S(1)}, bf16[128,1,64]{0,2,1:T(8,128)(2,1)}, u32[]{:S(2)}) copy-start(bf16[128,1,64]{0,2,1:T(8,128)(2,1)} %copy-done.10) | copy-start | bytes 49156
  152.1 16.2 %collective-permute-start.5 = (bf16[2,128,1,128]{1,3,2,0:T(8,128)(2,1)}, bf16[2,128,1,128]{1,3,2,0:T(8,128)(2,1)S(1)}, u32[]{:S(2)}, u32[]{:S(2)}) collective-permute-start(bf16[2,128,1,128]{1,3,2,0:T(8,128)(2,1)} %pad_maximum_fusion.1), channel_id=1, source_target_pairs={{0,24},{4,28},{8,32},{12,36},{16,40},{20,44},{24,48},{28,52},{32,5... | collective-permute-start | bytes 196616 | tf_op jit(solution)/shard_map/ppermute | solution.py:16
  156.2 12.4 %collective-permute-start.6 = (bf16[2,128,1,128]{1,3,2,0:T(8,128)(2,1)}, bf16[2,128,1,128]{1,3,2,0:T(8,128)(2,1)S(1)}, u32[]{:S(2)}, u32[]{:S(2)}) collective-permute-start(bf16[2,128,1,128]{1,3,2,0:T(8,128)(2,1)} %pad_maximum_fusion.1), channel_id=1, source_target_pairs={{0,28},{4,32},{8,36},{12,40},{16,44},{20,48},{24,52},{28,56},{32,6... | collective-permute-start | bytes 196616 | tf_op jit(solution)/shard_map/ppermute | solution.py:16
  161.9 7.3 %collective-permute-start.7 = (bf16[2,128,1,128]{1,3,2,0:T(8,128)(2,1)}, bf16[2,128,1,128]{1,3,2,0:T(8,128)(2,1)S(1)}, u32[]{:S(2)}, u32[]{:S(2)}) collective-permute-start(bf16[2,128,1,128]{1,3,2,0:T(8,128)(2,1)} %pad_maximum_fusion.1), channel_id=1, source_target_pairs={{0,32},{4,36},{8,40},{12,44},{16,48},{20,52},{24,56},{28,60},{32,6... | collective-permute-start | bytes 196616 | tf_op jit(solution)/shard_map/ppermute | solution.py:16
  172.1 3.7 copy-start.1
  175.8 1.2 copy-start.13
  178.4 4.1 copy-start.16
  178.4 4.1 copy-start.21
  182.4 72.4 %copy-start.14 = (f32[2560]{0:T(1024)S(1)}, f32[2560]{0:T(1024)}, u32[]{:S(2)}) copy-start(f32[2560]{0:T(1024)} %convert_element_type.149) | copy-start | bytes 30724
  182.4 258.7 %all-gather.11.cloned.1.call-start = ((), (), s32[]{:S(2)}) async-start(), calls=%async_computation.5 | async-start | bytes 3932160 | tf_op jit(solution)/shard_map/all_gather | solution.py:194
  265.3 130.5 %copy-start.27 = (bf16[1,2560,384]{2,1,0:T(8,128)(2,1)S(1)}, bf16[1,2560,384]{2,1,0:T(8,128)(2,1)}, u32[]{:S(2)}) copy-start(bf16[1,2560,384]{2,1,0:T(8,128)(2,1)} %param.27) | copy-start | bytes 5898244
  395.8 2.9 copy-start.28
  446.7 11.1 %copy-start.18 = (s32[1,128,6]{1,0,2:T(1,128)S(1)}, s32[1,128,6]{1,0,2:T(1,128)}, u32[]{:S(2)}) copy-start(s32[1,128,6]{1,0,2:T(1,128)} %param.25) | copy-start | bytes 9220
  446.7 11.3 %copy-start.23 = (f32[1,128,6]{1,0,2:T(1,128)S(1)}, f32[1,128,6]{1,0,2:T(1,128)}, u32[]{:S(2)}) copy-start(f32[1,128,6]{1,0,2:T(1,128)} %param.26) | copy-start | bytes 9220
  446.7 44.3 %all-to-all-start.1 = ((bf16[64,16,640]{2,1,0:T(8,128)(2,1)}), bf16[64,16,640]{2,1,0:T(8,128)(2,1)S(1)}, u32[]{:S(2)}, u32[]{:S(2)}) async-start(bf16[64,16,640]{2,1,0:T(8,128)(2,1)} %bitcast.201), calls=%async_computation.1 | async-start | bytes 2621440 | tf_op jit(solution)/shard_map/all_to_all | solution.py:201
Sparse Core Ops, SparseCore 0:
  9.2 22.2 all-gather.6
  52.1 18.4 all-gather.8
  182.5 69.9 all-reduce.1
  402.7 38.4 all-gather.10
where the time goes:
time: 507 us; the launch traced here: 506 us
  blocking collectives  232 us (46%)
  waiting for transfers between devices  139 us (27%)
  starting transfers between devices  40.3 us (8%)
  matrix products  34.8 us (7%)
  other arithmetic  25.5 us (5%)
  local copies, waits for them, and re-layouts  21 us (4%)
  between operations  13.8 us (3%)
    all_to_all x1, blocking collectives, on_device(): lax.all_to_all(outgoing, ('grp', 'tok'), split_axis=0, concat_axis=0, til...  131 us
    psum x1, waiting for transfers between devices, on_device(): lax.psum(partial_value.astype(jnp.bfloat16), 'head').astype(jnp.float32)  66.5 us
    all_gather x1, blocking collectives, on_device(): lax.all_gather(cached_prefix_values[0], 'tok', axis=0, tiled=True)  39.7 us
    all_gather x1, blocking collectives, on_device(): lax.all_gather(prefix_keys[0], 'tok', axis=0, tiled=True)  39.5 us
    all_gather x1, waiting for transfers between devices, on_device(): lax.all_gather(hidden, 'head', axis=1, tiled=True)  38.6 us
    all_to_all x1, waiting for transfers between devices, on_device(): lax.all_to_all(expert_out, ('grp', 'tok'), split_axis=0, concat_axis=0, t...  32.9 us
    ppermute x8, starting transfers between devices, shifted(): return lax.ppermute(block, axis, route)  29.3 us
    all_gather x1, blocking collectives, on_device(): features = lax.all_gather(quarter, 'head', axis=1, tiled=True)  13.2 us
  transfers between devices with their start and end apart: 13, of which 3 were waited for; matrix products, arithmetic and copies ran while one was open for 9% of the time, Pallas kernels for 0%

commit v1 on v0

v1 whole, which is shorter than its diff:
```python
import functools
import math

import jax
import jax.numpy as jnp
from jax import lax
from jax.experimental import pallas as pl
from jax.experimental.pallas import tpu as pltpu
from jax.sharding import PartitionSpec as P

ROPE_BASE = 500000.0
NORM_EPS = 1e-06
MASKED = -1e30
MESH = pl.DeviceIdType.MESH
Z, Y, X = 8, 4, 4
CHUNK_ORDER = (0, 1, 7, 2, 6, 3, 5, 4)
BACK = 2


class Copies:
    def __init__(self, send, recv):
        self.send, self.recv, self.made, self.open = send, recv, {}, []

    def start(self, key, src, dst, device):
        at = len(self.made)
        copy = pltpu.make_async_remote_copy(
            src_ref=src, dst_ref=dst, send_sem=self.send.at[at], recv_sem=self.recv.at[at],
            device_id=device, device_id_type=MESH,
        )
        copy.start()
        self.made[key] = copy
        self.open.append(key)

    def arrived(self, key):
        self.made[key].wait_recv()
        self.open.remove(key)

    def finish(self):
        for key in list(self.open):
            self.arrived(key)
        for copy in self.made.values():
            copy.wait_send()


def near(axis, step):
    if axis == "x":
        return {"head": lax.rem(lax.axis_index("head") + (step + X), X)}
    if axis == "core":
        return {"grp": 1 - lax.axis_index("grp")}
    tok = lax.axis_index("tok")
    z, y = tok // Y, lax.rem(tok, Y)
    if axis == "z":
        z = lax.rem(z + (step + Z), Z)
    else:
        y = lax.rem(y + (step + Y), Y)
    return {"tok": z * Y + y}


def greet(devices):
    barrier = pltpu.get_barrier_semaphore()
    for device in devices:
        pl.semaphore_signal(barrier, inc=1, device_id=device, device_id_type=MESH)
    pl.semaphore_wait(barrier, len(devices))


def torus_start(copies, kv, forward, backward):
    up, down = near("y", 1), near("y", -1)
    if forward:
        copies.start(("f", 1), kv.at[0, 0], kv.at[0, 1], near("z", 1))
    if backward:
        copies.start(("b", 1), kv.at[0, 0], kv.at[0, forward + backward], near("z", -1))
    copies.start(("u", 0), kv.at[0, 0], kv.at[1, 0], up)
    copies.start(("d", 0), kv.at[0, 0], kv.at[3, 0], down)


def torus_run(copies, kv, forward, backward):
    up, down = near("y", 1), near("y", -1)
    last = forward + backward
    for step in range(1, max(forward, backward) + 1):
        for mark, reach, slot, following, way in (
            ("f", forward, step, step + 1, 1),
            ("b", backward, last + 1 - step, last - step, -1),
        ):
            if step > reach:
                continue
            copies.arrived((mark, step))
            if step < reach:
                copies.start((mark, step + 1), kv.at[0, slot], kv.at[0, following], near("z", way))
            copies.start(("u", slot), kv.at[0, slot], kv.at[1, slot], up)
            copies.start(("d", slot), kv.at[0, slot], kv.at[3, slot], down)
    half = (last + 1) // 2
    for slot in range(last + 1):
        if slot <= half:
            copies.arrived(("u", slot))
            copies.start(("v", slot), kv.at[1, slot], kv.at[2, slot], up)
        else:
            copies.arrived(("d", slot))
            copies.start(("v", slot), kv.at[3, slot], kv.at[2, slot], down)


def torus_copies(forward, backward):
    slots = forward + backward + 1
    return forward + backward + 3 * slots


def ring_start(copies, key, ref, width, rows, offset):
    me = lax.axis_index("head")
    own = ref.at[pl.ds(offset, rows), pl.ds(pl.multiple_of(me * width, 128), width)]
    copies.start((key, "r"), own, own, near("x", 1))
    copies.start((key, "l"), own, own, near("x", -1))


def ring_relay(copies, key, ref, width, rows, offset):
    me = lax.axis_index("head")
    half = rows // 2
    copies.arrived((key, "r"))
    left = lax.rem(me + (X - 1), X)
    first = ref.at[pl.ds(offset, half), pl.ds(pl.multiple_of(left * width, 128), width)]
    copies.start((key, "rr"), first, first, near("x", 1))
    copies.arrived((key, "l"))
    right = lax.rem(me + 1, X)
    second = ref.at[pl.ds(offset + half, half), pl.ds(pl.multiple_of(right * width, 128), width)]
    copies.start((key, "ll"), second, second, near("x", -1))


def local(pairs, sems):
    made = [pltpu.make_async_copy(a, b, sems.at[i]) for i, (a, b) in enumerate(pairs)]
    for copy in made:
        copy.start()
    for copy in made:
        copy.wait()


VM = pl.BlockSpec(memory_space=pltpu.VMEM)
HB = pl.BlockSpec(memory_space=pl.ANY)


def call(kernel, ident, ins, outs, in_specs, out_specs, copies, extra=()):
    return pl.pallas_call(
        kernel,
        out_shape=outs,
        in_specs=in_specs,
        out_specs=out_specs,
        scratch_shapes=[
            pltpu.SemaphoreType.DMA((copies,)),
            pltpu.SemaphoreType.DMA((copies,)),
            pltpu.SemaphoreType.DMA((3,)),
            *extra,
        ],
        compiler_params=pltpu.CompilerParams(collective_id=ident, has_side_effects=True),
    )(*ins)


def shape(*dims, dtype=jnp.bfloat16):
    return jax.ShapeDtypeStruct(dims, dtype)


def prologue_kernel(hid, pk, pv, wq, wk, wv, wo, feat, kv, wq2, wk2, wv2, wo2, send, recv, sems):
    me = lax.axis_index("head")
    width = hid.shape[1]
    local(
        [
            (pk, kv.at[0, 0, 0]),
            (pv, kv.at[0, 0, 1]),
            (hid, feat.at[:, pl.ds(pl.multiple_of(me * width, 128), width)]),
        ],
        sems,
    )
    core = near("core", 1)
    greet([near("x", 1), near("x", -1), near("y", 1), near("y", -1), near("z", 1), near("z", -1), core])
    copies = Copies(send, recv)
    torus_start(copies, kv, 4, 3)
    ring_start(copies, "h", feat, width, hid.shape[0], 0)
    for key, a, b in (("q", wq, wq2), ("k", wk, wk2), ("w", wv, wv2), ("o", wo, wo2)):
        copies.start(key, a, b, core)
    torus_run(copies, kv, 4, 3)
    ring_relay(copies, "h", feat, width, hid.shape[0], 0)
    copies.finish()


def suffix_kernel(own, kv, send, recv, sems):
    local([(own, kv.at[0, 0])], sems)
    greet([near("y", 1), near("y", -1), near("z", 1), near("z", -1)])
    copies = Copies(send, recv)
    torus_start(copies, kv, BACK, 0)
    torus_run(copies, kv, BACK, 0)
    copies.finish()


def exchange_kernel(parts, got, send, recv, sems):
    me = lax.axis_index("head")
    greet([near("x", d) for d in range(1, X)])
    copies = Copies(send, recv)
    for d in (2, 1, 3):
        to = lax.rem(me + d, X)
        copies.start(d, parts.at[to], got.at[d - 1], near("x", d))
    copies.finish()


def small_kernel(block, got, send, recv, sems):
    greet([near("x", d) for d in range(1, X)])
    copies = Copies(send, recv)
    for d in (2, 1, 3):
        copies.start(d, block, got.at[d - 1], near("x", d))
    copies.finish()


def partner(slot, sign):
    tok = lax.axis_index("tok")
    grp = lax.axis_index("grp")
    dz, dy, dg = slot // 8, lax.rem(slot // 2, 4), lax.rem(slot, 2)
    z = lax.rem(tok // Y + Z + sign * dz, Z)
    y = lax.rem(lax.rem(tok, Y) + Y + sign * dy, Y)
    return {"grp": lax.rem(grp + dg, 2), "tok": z * Y + y}


def greet_all(more):
    barrier = pltpu.get_barrier_semaphore()

    def body(slot, carry):
        pl.semaphore_signal(barrier, inc=1, device_id=partner(slot, 1), device_id_type=MESH)
        return carry

    lax.fori_loop(1, 64, body, 0)
    for device in more:
        pl.semaphore_signal(barrier, inc=1, device_id=device, device_id_type=MESH)
    pl.semaphore_wait(barrier, 63 + len(more))


def dispatch_kernel(outgoing, rows, send, recv, sems, sent, came):
    me = lax.axis_index("head")
    width = outgoing.shape[1]
    cap = outgoing.shape[0] // 64
    columns = pl.ds(pl.multiple_of(me * width, 128), width)

    def copy_of(slot):
        at = pl.ds(pl.multiple_of(slot * cap, cap), cap)
        return pltpu.make_async_remote_copy(
            src_ref=outgoing.at[at, :], dst_ref=rows.at[at, columns],
            send_sem=sent.at[slot], recv_sem=came.at[slot],
            device_id=partner(slot, 1), device_id_type=MESH,
        )

    def start(slot, carry):
        copy_of(slot).start()
        return carry

    def wait_recv(slot, carry):
        copy_of(slot).wait_recv()
        return carry

    def wait_send(slot, carry):
        copy_of(slot).wait_send()
        return carry

    own = pltpu.make_async_copy(outgoing.at[pl.ds(0, cap), :], rows.at[pl.ds(0, cap), columns], sems.at[0])
    own.start()
    greet_all([near("x", 1), near("x", -1)])
    for chunk in CHUNK_ORDER:
        lax.fori_loop(max(8 * chunk, 1), 8 * chunk + 8, start, 0)
    own.wait()
    copies = Copies(send, recv)
    before = None
    for chunk in CHUNK_ORDER:
        lax.fori_loop(max(8 * chunk, 1), 8 * chunk + 8, wait_recv, 0)
        ring_start(copies, chunk, rows, width, 8 * cap, 8 * cap * chunk)
        if before is not None:
            ring_relay(copies, before, rows, width, 8 * cap, 8 * cap * before)
        before = chunk
    ring_relay(copies, before, rows, width, 8 * cap, 8 * cap * before)
    copies.finish()
    lax.fori_loop(1, 64, wait_send, 0)


def hidden_kernel(block, full, send, recv, sems):
    me = lax.axis_index("head")
    count, width = block.shape
    pieces = 4
    step = count // pieces
    own = pltpu.make_async_copy(
        block, full.at[:, pl.ds(pl.multiple_of(me * width, 128), width)], sems.at[0]
    )
    own.start()
    greet([near("x", 1), near("x", -1)])
    own.wait()
    copies = Copies(send, recv)
    for piece in range(pieces):
        ring_start(copies, piece, full, width, step, piece * step)
    for piece in range(pieces):
        ring_relay(copies, piece, full, width, step, piece * step)
    copies.finish()


def return_kernel(outputs, back, send, recv, sems, sent, came):
    cap = outputs.shape[0] // 64

    def copy_of(slot):
        at = pl.ds(pl.multiple_of(slot * cap, cap), cap)
        return pltpu.make_async_remote_copy(
            src_ref=outputs.at[at, :], dst_ref=back.at[at, :],
            send_sem=sent.at[slot], recv_sem=came.at[slot],
            device_id=partner(slot, -1), device_id_type=MESH,
        )

    def start(slot, carry):
        copy_of(slot).start()
        return carry

    def wait(slot, carry):
        copy_of(slot).wait()
        return carry

    own = pltpu.make_async_copy(outputs.at[pl.ds(0, cap), :], back.at[pl.ds(0, cap), :], sems.at[0])
    own.start()
    greet_all([])
    for chunk in CHUNK_ORDER:
        lax.fori_loop(max(8 * chunk, 1), 8 * chunk + 8, start, 0)
    own.wait()
    lax.fori_loop(1, 64, wait, 0)


def rms_norm(values_in, gain_vector):
    widened = values_in.astype(jnp.float32)
    mean_sq = jnp.mean(widened * widened, axis=-1, keepdims=True)
    return (widened * lax.rsqrt(mean_sq + NORM_EPS) * gain_vector.astype(jnp.float32)).astype(
        jnp.bfloat16
    )


def rotary_tables(token_positions, head_dim):
    half_dim = head_dim // 2
    frequency = jnp.exp(
        jnp.arange(half_dim, dtype=jnp.float32) * (-2.0 * math.log(ROPE_BASE) / head_dim)
    )
    angles = token_positions.astype(jnp.float32)[:, None] * frequency[None, :]
    return jnp.cos(angles), jnp.sin(angles)


def apply_rotary(product, cosine, sine_part):
    half_dim = product.shape[-1] // 2
    first_half = product[..., :half_dim]
    second_half = product[..., half_dim:]
    turned = jnp.concatenate(
        [
            first_half * cosine - second_half * sine_part,
            second_half * cosine + first_half * sine_part,
        ],
        axis=-1,
    )
    return turned.astype(jnp.bfloat16)


def attention_kernel(q, kv, sk, own_start, token_index, first, out):
    rows, dim = q.shape
    queries = q[...]
    scale = dim ** (-0.5)

    def step(state, keys, values, visible):
        top, total, summed = state
        scores = lax.dot_general(
            queries, keys, (((1,), (1,)), ((), ())), preferred_element_type=jnp.float32
        ) * scale
        if visible is not None:
            scores = jnp.where(visible, scores, MASKED)
        new_top = jnp.maximum(top, jnp.max(scores, axis=1, keepdims=True))
        weights = jnp.exp(scores - new_top)
        if visible is not None:
            weights = jnp.where(visible, weights, 0.0)
        factor = jnp.exp(top - new_top)
        total = total * factor + jnp.sum(weights, axis=1, keepdims=True)
        summed = summed * factor + jnp.dot(
            weights.astype(jnp.bfloat16), values, preferred_element_type=jnp.float32
        )
        return new_top, total, summed

    state = (
        jnp.full((rows, 1), MASKED, jnp.float32),
        jnp.zeros((rows, 1), jnp.float32),
        jnp.zeros((rows, dim), jnp.float32),
    )

    def prefix(index, state):
        return step(
            state,
            kv[index, :, 0].reshape(-1, dim),
            kv[index, :, 1].reshape(-1, dim),
            None,
        )

    state = lax.fori_loop(0, kv.shape[0], prefix, state)

    def suffix(index, state):
        keys = sk[index, :, 0].reshape(-1, dim)
        values = sk[index, :, 1].reshape(-1, dim)
        at = first[index, :][None, :]
        visible = (at >= own_start[...]) & (at <= token_index[...])
        return step(state, keys, values, visible)

    for index in range(sk.shape[0]):
        state = suffix(index, state)
    out[...] = (state[2] / state[1]).astype(out.dtype)


def on_device(
    hidden_in,
    attn_gain,
    w_query,
    key_projection_weight,
    value_projection_weight,
    w_out,
    prefix_keys,
    cached_prefix_values,
    request_lengths,
    moe_gain,
    expert_ids,
    route_weights,
    w_gate,
    w_up,
    w_down,
):
    f32, bf16 = jnp.float32, jnp.bfloat16
    tok_count = lax.axis_size("tok")
    tok_rank = lax.axis_index("tok")
    head_rank = lax.axis_index("head")
    grp_rank = lax.axis_index("grp")
    tok_dev = hidden_in.shape[1]
    model_width = attn_gain.shape[0]
    head_dim = prefix_keys.shape[3]
    prefix_dev = prefix_keys.shape[1]
    group_length = w_query.shape[1] // head_dim
    share = model_width // X
    quarter = hidden_in[0]

    features, prefix_kv, other_query, other_key, other_value, other_out = call(
        prologue_kernel, 0,
        (quarter, prefix_keys[0, :, 0], cached_prefix_values[0, :, 0], w_query,
         key_projection_weight, value_projection_weight, w_out),
        (shape(tok_dev, model_width), shape(Y, Z, 2, prefix_dev, head_dim), shape(*w_query.shape),
         shape(*key_projection_weight.shape), shape(*value_projection_weight.shape), shape(*w_out.shape)),
        [VM] * 3 + [HB] * 4, [VM] * 2 + [HB] * 4, torus_copies(4, 3) + 8,
    )
    attention_input = rms_norm(features, attn_gain)
    lengths = request_lengths[0]
    request_ends = jnp.cumsum(lengths)
    starts = request_ends - lengths
    token_index = tok_rank * tok_dev + jnp.arange(tok_dev, dtype=jnp.int32)
    own_start = jnp.max(
        jnp.where(starts[None, :] <= token_index[:, None], starts[None, :], 0), axis=1
    )
    token_positions = prefix_dev * tok_count + token_index - own_start
    cosine, sine_part = rotary_tables(token_positions, head_dim)

    half = model_width // 2
    lower = attention_input[:, :half]
    upper = attention_input[:, half:]
    mine = jnp.where(grp_rank == 0, lower, upper)
    others = jnp.where(grp_rank == 0, upper, lower)

    def project(own, other):
        return jnp.dot(mine, own, preferred_element_type=f32) + jnp.dot(
            others, other, preferred_element_type=f32
        )

    query_product = project(w_query, other_query).reshape(tok_dev, group_length, head_dim)
    key_product = project(key_projection_weight, other_key)
    value_product = project(value_projection_weight, other_value)
    queries = apply_rotary(
        jnp.transpose(query_product, (1, 0, 2)), cosine[None], sine_part[None]
    ).reshape(group_length * tok_dev, head_dim)
    suffix_own = jnp.stack(
        [apply_rotary(key_product, cosine, sine_part), value_product.astype(bf16)]
    )
    suffix_kv = call(
        suffix_kernel, 1, (suffix_own,), shape(Y, BACK + 1, 2, tok_dev, head_dim),
        [VM], VM, torus_copies(BACK, 0),
    )
    z_rank, y_rank = tok_rank // Y, tok_rank % Y
    y_from = (y_rank - jnp.arange(Y) + Y) % Y
    z_from = z_rank - jnp.arange(BACK + 1)
    device_from = jnp.where(z_from[None, :] >= 0, z_from[None, :] * Y + y_from[:, None], tok_count)
    key_index = (
        device_from[:, :, None] * tok_dev + jnp.arange(tok_dev, dtype=jnp.int32)
    ).reshape(Y, (BACK + 1) * tok_dev)
    rows = group_length * tok_dev
    attended = pl.pallas_call(
        attention_kernel,
        out_shape=shape(rows, head_dim),
        in_specs=[VM] * 6,
        out_specs=VM,
    )(
        queries, prefix_kv, suffix_kv,
        jnp.tile(own_start[:, None], (group_length, 1)),
        jnp.tile(token_index[:, None], (group_length, 1)),
        key_index.astype(jnp.int32),
    )
    attended = jnp.transpose(attended.reshape(group_length, tok_dev, head_dim), (1, 0, 2)).reshape(
        tok_dev, group_length * head_dim
    )

    def out_part(weights):
        return lax.dot_general(
            attended, weights, (((1,), (1,)), ((), ())), preferred_element_type=f32
        ).astype(bf16)

    own_part, other_part = out_part(w_out), out_part(other_out)
    first_part = jnp.where(grp_rank == 0, own_part, other_part)
    second_part = jnp.where(grp_rank == 0, other_part, own_part)
    parts = jnp.stack(
        [first_part[:, :share], first_part[:, share:], second_part[:, :share], second_part[:, share:]]
    )
    got = call(
        exchange_kernel, 2, (parts,), shape(X - 1, tok_dev, share), [VM], VM, X - 1
    )
    own_share = lax.dynamic_index_in_dim(parts, head_rank, 0, keepdims=False)
    mid = (
        quarter.astype(f32)
        + (own_share.astype(f32) + got[0].astype(f32) + got[1].astype(f32) + got[2].astype(f32))
    ).astype(bf16)
    mid_wide = mid.astype(f32)
    squares = jnp.sum(mid_wide * mid_wide, axis=1)
    small = jnp.broadcast_to(squares[None, :], (8, tok_dev))
    small_got = call(
        small_kernel, 3, (small,), shape(X - 1, 8, tok_dev, dtype=f32), [VM], VM, X - 1
    )
    mean_sq = (squares + small_got[0, 0] + small_got[1, 0] + small_got[2, 0]) / model_width
    gain = lax.dynamic_slice_in_dim(moe_gain, head_rank * share, share, 0).astype(f32)
    moe_in = (mid_wide * lax.rsqrt(mean_sq + NORM_EPS)[:, None] * gain).astype(bf16)

    experts = 2 * tok_count * w_gate.shape[0]
    top_count = expert_ids.shape[2]
    capacity = 4 * tok_dev * top_count // (3 * experts)
    chosen = expert_ids[0]
    e_grp, e_tok = chosen // tok_count, chosen % tok_count
    relative = (
        ((e_tok // Y - z_rank + Z) % Z) * 8
        + ((e_tok % Y - y_rank + Y) % Y) * 2
        + (e_grp + grp_rank) % 2
    )
    hit = relative[:, :, None] == jnp.arange(experts, dtype=jnp.int32)[None, None, :]
    uses = jnp.any(hit, axis=1)
    weight = jnp.sum(jnp.where(hit, route_weights[0][:, :, None], 0.0), axis=1)
    weight_hi = weight.astype(bf16)
    weight_lo = (weight - weight_hi.astype(f32)).astype(bf16)
    earlier = jnp.tril(jnp.ones((tok_dev, tok_dev), bf16), -1)
    rank = jnp.dot(earlier, uses.astype(bf16), preferred_element_type=f32)
    rank = jnp.where(uses, rank, -1.0).astype(bf16)
    slots = experts * capacity
    slot_index = jnp.arange(slots, dtype=jnp.int32)
    spread = (slot_index[None, :] // capacity == jnp.arange(experts, dtype=jnp.int32)[:, None]).astype(bf16)
    spread_rank = jnp.dot(rank, spread, preferred_element_type=f32)
    placed = spread_rank == (slot_index % capacity).astype(f32)[None, :]
    outgoing = lax.dot_general(
        placed.astype(bf16), moe_in, (((0,), (0,)), ((), ())), preferred_element_type=f32
    ).astype(bf16)

    flat_rows = call(
        dispatch_kernel, 4, (outgoing,), shape(slots, model_width), [VM], VM, 8 * 4,
        (pltpu.SemaphoreType.DMA((64,)), pltpu.SemaphoreType.DMA((64,))),
    )
    gate_act = jnp.dot(flat_rows, w_gate[0], preferred_element_type=f32)
    up_act = jnp.dot(flat_rows, w_up[0], preferred_element_type=f32)
    hidden = (jax.nn.silu(gate_act) * up_act).astype(bf16)
    full_hidden = call(
        hidden_kernel, 5, (hidden,), shape(slots, X * hidden.shape[1]), [VM], VM, 4 * 4
    )
    expert_out = jnp.dot(full_hidden, w_down[0], preferred_element_type=f32).astype(bf16)
    returned = call(
        return_kernel, 6, (expert_out,), shape(slots, share), [VM], VM, 1,
        (pltpu.SemaphoreType.DMA((64,)), pltpu.SemaphoreType.DMA((64,))),
    )

    def combine(part):
        spread_weight = jnp.where(placed, jnp.dot(part, spread, preferred_element_type=f32), 0.0)
        return jnp.dot(spread_weight.astype(bf16), returned, preferred_element_type=f32)

    output = (mid_wide + (combine(weight_hi) + combine(weight_lo))).astype(bf16)
    return output[None]


def solution(mesh):
    return jax.shard_map(
        on_device,
        mesh=mesh,
        in_specs=(
            P("grp", "tok", "head"),
            P(),
            P("grp", "head"),
            P("grp", "head"),
            P("grp", "head"),
            P("grp", "head"),
            P("grp", "tok", "head", None),
            P("grp", "tok", "head", None),
            P("grp", None),
            P(),
            P("grp", "tok", None),
            P("grp", "tok", None),
            P(("grp", "tok"), None, "head"),
            P(("grp", "tok"), None, "head"),
            P(("grp", "tok"), None, "head"),
        ),
        out_specs=P("grp", "tok", "head"),
        check_vma=False,
    )
```

time: 507 us -> 262 us (0.52)
  blocking collectives: 232 us -> 0 us
  Pallas kernels: 0 us -> 213 us
  waiting for transfers between devices: 139 us -> 0 us
  starting transfers between devices: 40.3 us -> 0 us
  local copies, waits for them, and re-layouts: 21 us -> 5.04 us
  other arithmetic: 25.5 us -> 10.5 us
  between operations: 13.8 us -> 0.43 us
    pallas_call x0 -> x8, Pallas kernels: none -> 213 us  [the longest x7 204 us: call(): pl.pallas_call(kernel, out_shape=outs, in_specs=in_specs, out_specs=out_s...]
    all_to_all x1 -> x0, blocking collectives: 131 us -> none  [on_device(): lax.all_to_all(outgoing, ('grp', 'tok'), split_axis=0, concat_axis=0, til...]
    all_gather x5 -> x0, blocking collectives: 101 us -> none  [the longest x1 39.7 us: on_device(): lax.all_gather(cached_prefix_values[0], 'tok', axis=0, tiled=True)]
    psum x1 -> x0, waiting for transfers between devices: 66.5 us -> none  [on_device(): lax.psum(partial_value.astype(jnp.bfloat16), 'head').astype(jnp.float32)]
    all_gather x3 -> x0, waiting for transfers between devices: 38.6 us -> none  [the longest x1 38.6 us: on_device(): lax.all_gather(hidden, 'head', axis=1, tiled=True)]
    all_to_all x1 -> x0, waiting for transfers between devices: 32.9 us -> none  [on_device(): lax.all_to_all(expert_out, ('grp', 'tok'), split_axis=0, concat_axis=0, t...]
    ppermute x8 -> x0, starting transfers between devices: 29.3 us -> none  [shifted(): return lax.ppermute(block, axis, route)]
    gather x3 -> x0, local copies, waits for them, and re-layouts: 11.8 us -> none  [the longest x1 6.31 us: on_device(): jnp.take(moe_in, source, axis=0, mode='fill', fill_value=0)]
  transfers between devices with their start and end apart: 13 -> 0, of which waited for: 3 -> 0; matrix products, arithmetic and copies ran while one was open for 9% -> 0% of each run, Pallas kernels for 0% -> 0%
where the time goes in v1:
time: 262 us; the launch traced here: 260 us
  Pallas kernels  213 us (81%)
  matrix products  31.3 us (12%)
  other arithmetic  10.5 us (4%)
  local copies, waits for them, and re-layouts  5.04 us (2%)
    pallas_call x7, Pallas kernels, call(): pl.pallas_call(kernel, out_shape=outs, in_specs=in_specs, out_specs=out_s...  204 us
    pallas_call x1, Pallas kernels, on_device(): pl.pallas_call(attention_kernel, out_shape=shape(rows, head_dim), in_spec...  8.57 us
    dot_general x1, matrix products, on_device(): gate_act = jnp.dot(flat_rows, w_gate[0], preferred_element_type=f32)  5.72 us
    dot_general x1, matrix products, on_device(): jnp.dot(full_hidden, w_down[0], preferred_element_type=f32).astype(bf16)  5.57 us

profile of v1, /device:TPU:1, one launch (start us, length us, event | category | flops | bytes accessed | tf_op | source)
XLA Modules:
  0.0 260.0 jit_solution(17005177910981345415)
XLA Ops:
  0.0 27.0 %shard_map.145 = (bf16[128,2560]{1,0:T(8,128)(2,1)}, bf16[4,8,2,64,128]{4,3,2,1,0:T(8,128)(2,1)}, bf16[1280,640]{1,0:T(8,128)(2,1)}, bf16[1280,128]{1,0:T(8,128)...) custom-call(bf16[128,640]{1,0:T(8,128)(2,1)} %bitcast.138, bf16[64,128]{1,0:T(8,128)(2,1)} %bitcast.141, ...), custom_call_target="tpu_custom_call" | custom-call | tf_op jit(solution)/shard_map/pallas_call | solution.py:139
  27.0 1.3 fusion.11
  28.3 1.3 fusion.13
  29.7 1.2 fusion.93
  30.9 1.2 convolution_add_fusion.3
  32.2 0.2 reduce-window_clone.1
  32.4 0.1 select_reduce_fusion.1
  32.5 0.3 fusion.43
  32.8 0.1 copy.34
  32.9 0.1 copy.35
  32.9 0.0 copy-start.4
  33.0 2.0 fusion.92
  35.0 0.4 convolution_add_fusion.1
  35.4 0.9 copy.33
  36.3 1.0 subtract_convert_fusion
  37.3 0.2 copy.36
  37.5 0.2 copy.37
  37.7 0.8 pad_maximum_fusion.1.q
  38.5 0.1 select_multiply_fusion
  38.6 0.7 bitcast_add_fusion.1.first
  39.3 0.2 fusion.94
  39.5 1.2 fusion.21
  40.7 0.7 pad_maximum_fusion.2.own
  41.4 13.4 %shard_map.146.sk = bf16[4,3,2,128,128]{4,3,2,1,0:T(8,128)(2,1)} custom-call(bf16[2,128,128]{2,1,0:T(8,128)(2,1)} %pad_maximum_fusion.2.own), custom_call_target="tpu_custom_call" | custom-call | tf_op jit(solution)/shard_map/pallas_call | solution.py:139
  54.9 0.9 copy.48
  55.8 0.9 copy.50
  56.7 8.6 %shard_map.147 = bf16[640,128]{1,0:T(8,128)(2,1)} custom-call(bf16[640,128]{1,0:T(8,128)(2,1)} %pad_maximum_fusion.1.q, bf16[4,8,2,64,128]{4,3,2,1,0:T(8,128)(2,1)} %get-tuple-element.13.kv, bf16[4,3,2,128,128]{4,3,2,1,0:T(8,128)(2,1)} %shard_map.146.sk, s32[640,1]{1,0:T(8,128)} %bitcast.134, s32[640,1]{1,0:T(8,128)} %bitcast.135, ...), custom_call_target="tpu_custom_call" | custom-call | tf_op jit(solution)/shard_map/pallas_call | solution.py:485
  65.3 1.1 copy.42
  66.4 2.2 convolution_convert_fusion
  68.5 0.6 broadcast_select_fusion.1
  69.2 0.1 slice_bitcast_fusion.1
  69.3 0.9 pad_maximum_fusion.parts
  70.2 10.0 %shard_map.148 = bf16[3,128,640]{2,1,0:T(8,128)(2,1)} custom-call(bf16[4,128,640]{2,1,0:T(8,128)(2,1)} %pad_maximum_fusion.parts), custom_call_target="tpu_custom_call" | custom-call | tf_op jit(solution)/shard_map/pallas_call | solution.py:139
  80.2 1.4 fusion.23
  81.6 0.6 broadcast_in_dim.92.block
  82.2 5.5 %shard_map.149 = f32[3,8,128]{2,1,0:T(8,128)} custom-call(f32[8,128]{1,0:T(8,128)} %broadcast_in_dim.92.block), custom_call_target="tpu_custom_call" | custom-call | tf_op jit(solution)/shard_map/pallas_call | solution.py:139
  87.7 0.7 fusion.83
  88.5 0.5 convolution_compare_fusion
  89.0 0.8 dynamic-slice_convert_fusion
  89.8 1.7 convolution_convert_fusion.2.outgoing
  91.5 74.6 %shard_map.150 = bf16[1024,2560]{1,0:T(8,128)(2,1)} custom-call(bf16[1024,640]{1,0:T(8,128)(2,1)} %convolution_convert_fusion.2.outgoing), custom_call_target="tpu_custom_call" | custom-call | tf_op jit(solution)/shard_map/pallas_call | solution.py:139
  166.2 5.7 %fusion.4 = f32[1024,384]{1,0:T(8,128)S(1)} fusion(bf16[1024,2560]{1,0:T(8,128)(2,1)} %shard_map.150, bf16[1,2560,384]{2,1,0:T(8,128)(2,1)} %param.27), kind=kOutput, calls=%fused_computation.6 | convolution fusion | flops 2013265920 | bytes 8781824 | tf_op jit(solution)/shard_map/dot_general | solution.py:560
  171.9 3.8 %multiply_convert_fusion.block = bf16[1024,384]{1,0:T(8,128)(2,1)} fusion(f32[1024,384]{1,0:T(8,128)S(1)} %fusion.4, bf16[1024,2560]{1,0:T(8,128)(2,1)S(1)} %copy-done.3, bf16[1,2560,384]{2,1,0:T(8,128)(2,1)S(1)} %copy-done.11), kind=kOutput, calls=%fused_computation.12 | convolution fusion | flops 2015625216 | bytes 9568256 | tf_op jit(solution)/shard_map/dot_general | solution.py:561
  175.7 31.5 %shard_map.151 = bf16[1024,1536]{1,0:T(8,128)(2,1)} custom-call(bf16[1024,384]{1,0:T(8,128)(2,1)} %multiply_convert_fusion.block), custom_call_target="tpu_custom_call" | custom-call | tf_op jit(solution)/shard_map/pallas_call | solution.py:139
  207.2 5.6 %fusion.6.outputs = bf16[1024,640]{1,0:T(8,128)(2,1)} fusion(bf16[1024,1536]{1,0:T(8,128)(2,1)} %shard_map.151, bf16[1,1536,640]{2,1,0:T(8,128)(2,1)S(1)} %copy-done), kind=kOutput, calls=%fused_computation.11 | convolution fusion | flops 2013921280 | bytes 6422528 | tf_op jit(solution)/shard_map/dot_general | solution.py:566
  212.8 42.2 %shard_map.152 = bf16[1024,640]{1,0:T(8,128)(2,1)} custom-call(bf16[1024,640]{1,0:T(8,128)(2,1)} %fusion.6.outputs), custom_call_target="tpu_custom_call" | custom-call | tf_op jit(solution)/shard_map/pallas_call | solution.py:139
  255.1 2.7 %fusion.17 = f32[128,640]{1,0:T(8,128)} fusion(bf16[1024,640]{1,0:T(8,128)(2,1)} %shard_map.152, pred[128,1024]{1,0:T(32,128)(4,1)} %copy-done.6, s32[1024]{0:T(1024)S(1)} %get-tuple-element.33, f32[128,64]{0,1:T(8,128)S(1)} %select_reduce_fusion), kind=kOutput, calls=%fused_computation.24 | convolution fusion | flops 184885248 | bytes 1806336 | tf_op jit(solution)/shard_map/dot_general | solution.py:574
  257.8 2.2 fusion.19
  (46 shorter events, 0.3 us)
Async XLA Ops:
  0.0 207.2 %copy-start = (bf16[1,1536,640]{2,1,0:T(8,128)(2,1)S(1)}, bf16[1,1536,640]{2,1,0:T(8,128)(2,1)}, u32[]{:S(2)}) copy-start(bf16[1,1536,640]{2,1,0:T(8,128)(2,1)} %param.29) | copy-start | bytes 5898244
  0.0 28.3 %copy-start.8 = (bf16[2560]{0:T(1024)(128)(2,1)S(1)}, bf16[2560]{0:T(1024)(128)(2,1)}, u32[]{:S(2)}) copy-start(bf16[2560]{0:T(1024)(128)(2,1)} %param.16) | copy-start | bytes 15364
  29.6 2.5 copy-start.12
  32.9 2.0 copy-start.4
  35.4 3.9 %copy-start.5 = (bf16[1280,128]{1,0:T(8,128)(2,1)S(1)}, bf16[1280,128]{1,0:T(8,128)(2,1)}, u32[]{:S(2)}) copy-start(bf16[1280,128]{1,0:T(8,128)(2,1)} %wv.1) | copy-start | bytes 983044
  66.4 2.2 copy-start.2
  69.2 11.1 %copy-start.7 = (bf16[1,128,640]{2,1,0:T(8,128)(2,1)S(1)}, bf16[1,128,640]{2,1,0:T(8,128)(2,1)}, u32[]{:S(2)}) copy-start(bf16[1,128,640]{2,1,0:T(8,128)(2,1)} %param.15) | copy-start | bytes 491524
  69.2 19.1 %copy-start.10 = (s32[1,128,6]{1,0,2:T(1,128)S(1)}, s32[1,128,6]{1,0,2:T(1,128)}, u32[]{:S(2)}) copy-start(s32[1,128,6]{1,0,2:T(1,128)} %param.25) | copy-start | bytes 9220
  89.0 77.1 %copy-start.6 = (pred[128,1024]{1,0:T(32,128)(4,1)}, pred[128,1024]{1,0:T(32,128)(4,1)S(1)}, u32[]{:S(2)}) copy-start(pred[128,1024]{1,0:T(32,128)(4,1)S(1)} %convolution_compare_fusion) | copy-start | bytes 393220
  166.1 5.8 %copy-start.3 = (bf16[1024,2560]{1,0:T(8,128)(2,1)S(1)}, bf16[1024,2560]{1,0:T(8,128)(2,1)}, u32[]{:S(2)}) copy-start(bf16[1024,2560]{1,0:T(8,128)(2,1)} %shard_map.150) | copy-start | bytes 15728644
  166.1 5.8 %copy-start.11 = (bf16[1,2560,384]{2,1,0:T(8,128)(2,1)S(1)}, bf16[1,2560,384]{2,1,0:T(8,128)(2,1)}, u32[]{:S(2)}) copy-start(bf16[1,2560,384]{2,1,0:T(8,128)(2,1)} %param.28) | copy-start | bytes 5898244
  212.8 42.2 %copy-start.9 = (f32[1,128,6]{1,0,2:T(1,128)S(1)}, f32[1,128,6]{1,0,2:T(1,128)}, u32[]{:S(2)}) copy-start(f32[1,128,6]{1,0,2:T(1,128)} %param.26) | copy-start | bytes 9220
  255.0 2.8 %copy-start.1 = (bf16[1024,640]{1,0:T(8,128)(2,1)S(1)}, bf16[1024,640]{1,0:T(8,128)(2,1)}, u32[]{:S(2)}) copy-start(bf16[1024,640]{1,0:T(8,128)(2,1)} %shard_map.152) | copy-start | bytes 3932164

commit v2 on v1

--- a/solution.py
+++ b/solution.py
@@ -13,7 +13,7 @@
 MASKED = -1e30
 MESH = pl.DeviceIdType.MESH
 Z, Y, X = 8, 4, 4
-CHUNK_ORDER = (0, 1, 7, 2, 6, 3, 5, 4)
+CHUNK_ORDER = (0, 1, 5, 3, 4, 6, 2, 7)
 BACK = 2
 
 
@@ -144,7 +144,7 @@
         scratch_shapes=[
             pltpu.SemaphoreType.DMA((copies,)),
             pltpu.SemaphoreType.DMA((copies,)),
-            pltpu.SemaphoreType.DMA((3,)),
+            pltpu.SemaphoreType.DMA((4,)),
             *extra,
         ],
         compiler_params=pltpu.CompilerParams(collective_id=ident, has_side_effects=True),
@@ -227,96 +227,106 @@
     pl.semaphore_wait(barrier, 63 + len(more))
 
 
-def dispatch_kernel(outgoing, rows, send, recv, sems, sent, came):
+def experts_kernel(
+    outgoing, w_gate, w_up, w_down, back,
+    send, recv, sems, sent, came, sent_back, came_back, rows, hidden, results, wide, down,
+):
     me = lax.axis_index("head")
     width = outgoing.shape[1]
     cap = outgoing.shape[0] // 64
+    inner = w_gate.shape[1]
+    many = 8 * cap
     columns = pl.ds(pl.multiple_of(me * width, 128), width)
-
-    def copy_of(slot):
-        at = pl.ds(pl.multiple_of(slot * cap, cap), cap)
+    own_hidden = pl.ds(pl.multiple_of(me * inner, 128), inner)
+
+    def block(slot):
+        return pl.ds(pl.multiple_of(slot * cap, cap), cap)
+
+    def there(slot):
         return pltpu.make_async_remote_copy(
-            src_ref=outgoing.at[at, :], dst_ref=rows.at[at, columns],
+            src_ref=outgoing.at[block(slot), :], dst_ref=rows.at[block(slot), columns],
             send_sem=sent.at[slot], recv_sem=came.at[slot],
             device_id=partner(slot, 1), device_id_type=MESH,
         )
 
-    def start(slot, carry):
-        copy_of(slot).start()
-        return carry
-
-    def wait_recv(slot, carry):
-        copy_of(slot).wait_recv()
-        return carry
-
-    def wait_send(slot, carry):
-        copy_of(slot).wait_send()
-        return carry
-
-    own = pltpu.make_async_copy(outgoing.at[pl.ds(0, cap), :], rows.at[pl.ds(0, cap), columns], sems.at[0])
+    def home(slot):
+        return pltpu.make_async_remote_copy(
+            src_ref=results.at[block(slot), :], dst_ref=back.at[block(slot), :],
+            send_sem=sent_back.at[slot], recv_sem=came_back.at[slot],
+            device_id=partner(slot, -1), device_id_type=MESH,
+        )
+
+    def each(first, last, act):
+        def body(slot, carry):
+            act(slot)
+            return carry
+
+        lax.fori_loop(first, last, body, 0)
+
+    def of_chunk(chunk, act):
+        each(max(8 * chunk, 1), 8 * chunk + 8, act)
+
+    weights = [
+        pltpu.make_async_copy(w_gate, wide.at[:, pl.ds(0, inner)], sems.at[0]),
+        pltpu.make_async_copy(w_up, wide.at[:, pl.ds(inner, inner)], sems.at[1]),
+        pltpu.make_async_copy(w_down, down, sems.at[2]),
+    ]
+    own = pltpu.make_async_copy(outgoing.at[block(0), :], rows.at[block(0), columns], sems.at[3])
     own.start()
+    for copy in weights:
+        copy.start()
     greet_all([near("x", 1), near("x", -1)])
     for chunk in CHUNK_ORDER:
-        lax.fori_loop(max(8 * chunk, 1), 8 * chunk + 8, start, 0)
+        of_chunk(chunk, lambda slot: there(slot).start())
     own.wait()
+    for copy in weights:
+        copy.wait()
     copies = Copies(send, recv)
-    before = None
-    for chunk in CHUNK_ORDER:
-        lax.fori_loop(max(8 * chunk, 1), 8 * chunk + 8, wait_recv, 0)
-        ring_start(copies, chunk, rows, width, 8 * cap, 8 * cap * chunk)
-        if before is not None:
-            ring_relay(copies, before, rows, width, 8 * cap, 8 * cap * before)
-        before = chunk
-    ring_relay(copies, before, rows, width, 8 * cap, 8 * cap * before)
+    last = pltpu.make_async_copy(results.at[block(0), :], back.at[block(0), :], sems.at[3])
+
+    def arrive(chunk):
+        of_chunk(chunk, lambda slot: there(slot).wait_recv())
+        ring_start(copies, ("m", chunk), rows, width, many, many * chunk)
+
+    def pass_rows(chunk):
+        ring_relay(copies, ("m", chunk), rows, width, many, many * chunk)
+
+    def gate_up(chunk):
+        copies.arrived((("m", chunk), "rr"))
+        copies.arrived((("m", chunk), "ll"))
+        at = pl.ds(many * chunk, many)
+        both = jnp.dot(rows[at, :], wide[...], preferred_element_type=jnp.float32)
+        gate = both[:, :inner]
+        hidden[at, own_hidden] = (gate / (1.0 + jnp.exp(-gate)) * both[:, inner:]).astype(hidden.dtype)
+
+    def send_hidden(chunk):
+        of_chunk(chunk, lambda slot: there(slot).wait_send())
+        ring_start(copies, ("h", chunk), hidden, inner, many, many * chunk)
+
+    def pass_hidden(chunk):
+        ring_relay(copies, ("h", chunk), hidden, inner, many, many * chunk)
+
+    def finish(chunk):
+        copies.arrived((("h", chunk), "rr"))
+        copies.arrived((("h", chunk), "ll"))
+        at = pl.ds(many * chunk, many)
+        results[at, :] = jnp.dot(
+            hidden[at, :], down[...], preferred_element_type=jnp.float32
+        ).astype(results.dtype)
+
+    def send_home(chunk):
+        if chunk == 0:
+            last.start()
+        of_chunk(chunk, lambda slot: home(slot).start())
+
+    stages = ((arrive, 0), (pass_rows, 1), (gate_up, 2), (pass_hidden, 3), (send_hidden, 2), (send_home, 5), (finish, 4))
+    for step in range(len(CHUNK_ORDER) + 5):
+        for stage, lag in stages:
+            if 0 <= step - lag < len(CHUNK_ORDER):
+                stage(CHUNK_ORDER[step - lag])
     copies.finish()
-    lax.fori_loop(1, 64, wait_send, 0)
-
-
-def hidden_kernel(block, full, send, recv, sems):
-    me = lax.axis_index("head")
-    count, width = block.shape
-    pieces = 4
-    step = count // pieces
-    own = pltpu.make_async_copy(
-        block, full.at[:, pl.ds(pl.multiple_of(me * width, 128), width)], sems.at[0]
-    )
-    own.start()
-    greet([near("x", 1), near("x", -1)])
-    own.wait()
-    copies = Copies(send, recv)
-    for piece in range(pieces):
-        ring_start(copies, piece, full, width, step, piece * step)
-    for piece in range(pieces):
-        ring_relay(copies, piece, full, width, step, piece * step)
-    copies.finish()
-
-
-def return_kernel(outputs, back, send, recv, sems, sent, came):
-    cap = outputs.shape[0] // 64
-
-    def copy_of(slot):
-        at = pl.ds(pl.multiple_of(slot * cap, cap), cap)
-        return pltpu.make_async_remote_copy(
-            src_ref=outputs.at[at, :], dst_ref=back.at[at, :],
-            send_sem=sent.at[slot], recv_sem=came.at[slot],
-            device_id=partner(slot, -1), device_id_type=MESH,
-        )
-
-    def start(slot, carry):
-        copy_of(slot).start()
-        return carry
-
-    def wait(slot, carry):
-        copy_of(slot).wait()
-        return carry
-
-    own = pltpu.make_async_copy(outputs.at[pl.ds(0, cap), :], back.at[pl.ds(0, cap), :], sems.at[0])
-    own.start()
-    greet_all([])
-    for chunk in CHUNK_ORDER:
-        lax.fori_loop(max(8 * chunk, 1), 8 * chunk + 8, start, 0)
-    own.wait()
-    lax.fori_loop(1, 64, wait, 0)
+    last.wait()
+    each(1, 64, lambda slot: home(slot).wait())
 
 
 def rms_norm(values_in, gain_vector):
@@ -553,20 +563,18 @@
         placed.astype(bf16), moe_in, (((0,), (0,)), ((), ())), preferred_element_type=f32
     ).astype(bf16)
 
-    flat_rows = call(
-        dispatch_kernel, 4, (outgoing,), shape(slots, model_width), [VM], VM, 8 * 4,
-        (pltpu.SemaphoreType.DMA((64,)), pltpu.SemaphoreType.DMA((64,))),
-    )
-    gate_act = jnp.dot(flat_rows, w_gate[0], preferred_element_type=f32)
-    up_act = jnp.dot(flat_rows, w_up[0], preferred_element_type=f32)
-    hidden = (jax.nn.silu(gate_act) * up_act).astype(bf16)
-    full_hidden = call(
-        hidden_kernel, 5, (hidden,), shape(slots, X * hidden.shape[1]), [VM], VM, 4 * 4
-    )
-    expert_out = jnp.dot(full_hidden, w_down[0], preferred_element_type=f32).astype(bf16)
+    inner = w_gate.shape[2]
     returned = call(
-        return_kernel, 6, (expert_out,), shape(slots, share), [VM], VM, 1,
-        (pltpu.SemaphoreType.DMA((64,)), pltpu.SemaphoreType.DMA((64,))),
+        experts_kernel, 4, (outgoing, w_gate[0], w_up[0], w_down[0]), shape(slots, share),
+        [VM] + [HB] * 3, VM, 2 * 8 * 4,
+        (
+            *[pltpu.SemaphoreType.DMA((64,))] * 4,
+            pltpu.VMEM((slots, model_width), bf16),
+            pltpu.VMEM((slots, X * inner), bf16),
+            pltpu.VMEM((slots, share), bf16),
+            pltpu.VMEM((model_width, 2 * inner), bf16),
+            pltpu.VMEM((X * inner, share), bf16),
+        ),
     )
 
     def combine(part):

time: 262 us -> 209 us (0.80)
  Pallas kernels: 213 us -> 183 us
  matrix products: 31.3 us -> 9.37 us
    pallas_call x7 -> x5, Pallas kernels: 204 us -> 175 us  [call(): pl.pallas_call(kernel, out_shape=outs, in_specs=in_specs, out_specs=out_s...]
    dot_general x3 -> x0, matrix products: 15.1 us -> none  [the longest x1 5.72 us: on_device(): gate_act = jnp.dot(flat_rows, w_gate[0], preferred_element_type=f32)]
where the time goes in v2:
time: 209 us; the launch traced here: 208 us
  Pallas kernels  183 us (88%)
  other arithmetic  9.51 us (5%)
  matrix products  9.37 us (4%)
  local copies, waits for them, and re-layouts  5.42 us (3%)
    pallas_call x5, Pallas kernels, call(): pl.pallas_call(kernel, out_shape=outs, in_specs=in_specs, out_specs=out_s...  175 us
    pallas_call x1, Pallas kernels, on_device(): pl.pallas_call(attention_kernel, out_shape=shape(rows, head_dim), in_spec...  8.69 us

profile of v2, /device:TPU:1, one launch (start us, length us, event | category | flops | bytes accessed | tf_op | source)
XLA Modules:
  0.0 208.2 jit_solution(14126279061668297666)
XLA Ops:
  0.0 26.8 %shard_map.145 = (bf16[128,2560]{1,0:T(8,128)(2,1)}, bf16[4,8,2,64,128]{4,3,2,1,0:T(8,128)(2,1)}, bf16[1280,640]{1,0:T(8,128)(2,1)}, bf16[1280,128]{1,0:T(8,128)...) custom-call(bf16[128,640]{1,0:T(8,128)(2,1)} %bitcast.128, bf16[64,128]{1,0:T(8,128)(2,1)} %bitcast.131, ...), custom_call_target="tpu_custom_call" | custom-call | tf_op jit(solution)/shard_map/pallas_call | solution.py:139
  26.8 0.0 copy-start.5
  26.9 1.3 fusion
  28.2 1.3 fusion.2
  29.5 0.0 copy-start.12
  29.6 0.2 fusion.82
  29.9 1.4 convolution_add_fusion.3
  31.3 0.2 reduce-window_clone.1
  31.5 0.1 select_reduce_fusion.1
  31.6 0.3 fusion.32
  31.9 0.1 copy.34
  32.0 0.1 copy.35
  32.1 0.0 copy-done.2
  32.1 0.4 fusion.81
  32.5 1.0 copy-done.4
  33.5 0.4 convolution_add_fusion.1
  34.0 0.0 copy-start.6
  34.0 0.2 copy.33
  34.1 0.1 subtract_convert_fusion
  34.2 0.2 copy.36
  34.4 0.2 copy.37
  34.5 0.8 pad_maximum_fusion.1.q
  35.4 0.1 select_multiply_fusion
  35.5 0.7 bitcast_add_fusion.1.first
  36.1 0.2 fusion.83
  36.4 0.2 fusion.10
  36.6 0.7 pad_maximum_fusion.2.own
  37.3 13.4 %shard_map.146.sk = bf16[4,3,2,128,128]{4,3,2,1,0:T(8,128)(2,1)} custom-call(bf16[2,128,128]{2,1,0:T(8,128)(2,1)} %pad_maximum_fusion.2.own), custom_call_target="tpu_custom_call" | custom-call | tf_op jit(solution)/shard_map/pallas_call | solution.py:139
  50.8 0.9 copy.48
  51.7 0.9 copy.50
  52.6 8.7 %shard_map.147 = bf16[640,128]{1,0:T(8,128)(2,1)} custom-call(bf16[640,128]{1,0:T(8,128)(2,1)} %pad_maximum_fusion.1.q, bf16[4,8,2,64,128]{4,3,2,1,0:T(8,128)(2,1)} %get-tuple-element.13.kv, bf16[4,3,2,128,128]{4,3,2,1,0:T(8,128)(2,1)} %shard_map.146.sk, s32[640,1]{1,0:T(8,128)} %bitcast.124, s32[640,1]{1,0:T(8,128)} %bitcast.125, ...), custom_call_target="tpu_custom_call" | custom-call | tf_op jit(solution)/shard_map/pallas_call | solution.py:495
  61.3 1.2 copy.42
  62.5 0.6 convolution_convert_fusion
  63.1 0.6 broadcast_select_fusion.1
  63.8 0.0 copy-start.7
  63.8 0.1 slice_bitcast_fusion.1
  63.9 0.9 pad_maximum_fusion.parts
  64.8 10.0 %shard_map.148 = bf16[3,128,640]{2,1,0:T(8,128)(2,1)} custom-call(bf16[4,128,640]{2,1,0:T(8,128)(2,1)} %pad_maximum_fusion.parts), custom_call_target="tpu_custom_call" | custom-call | tf_op jit(solution)/shard_map/pallas_call | solution.py:139
  74.8 1.4 fusion.12
  76.2 0.6 broadcast_in_dim.92.block
  76.8 5.5 %shard_map.149 = f32[3,8,128]{2,1,0:T(8,128)} custom-call(f32[8,128]{1,0:T(8,128)} %broadcast_in_dim.92.block), custom_call_target="tpu_custom_call" | custom-call | tf_op jit(solution)/shard_map/pallas_call | solution.py:139
  82.3 0.7 fusion.72
  83.1 0.5 convolution_compare_fusion
  83.6 0.8 dynamic-slice_convert_fusion
  84.4 1.6 convolution_convert_fusion.2.outgoing
  86.0 119.0 %shard_map.150 = bf16[1024,640]{1,0:T(8,128)(2,1)} custom-call(bf16[1024,640]{1,0:T(8,128)(2,1)} %convolution_convert_fusion.2.outgoing, bf16[2560,384]{1,0:T(8,128)(2,1)} %bitcast.119, bf16[2560,384]{1,0:T(8,128)(2,1)} %bitcast.120, bf16[1536,640]{1,0:T(8,128)(2,1)} %bitcast.121), custom_call_target="tpu_custom_call" | custom-call | tf_op jit(solution)/shard_map/pallas_call | solution.py:139
  205.0 1.9 fusion.6
  207.0 1.2 fusion.8
  (41 shorter events, 0.3 us)
Async XLA Ops:
  0.0 28.2 %copy-start.9 = (bf16[2560]{0:T(1024)(128)(2,1)S(1)}, bf16[2560]{0:T(1024)(128)(2,1)}, u32[]{:S(2)}) copy-start(bf16[2560]{0:T(1024)(128)(2,1)} %param.16) | copy-start | bytes 15364
  26.8 2.8 %copy-start.5 = (bf16[1280,128]{1,0:T(8,128)(2,1)S(1)}, bf16[1280,128]{1,0:T(8,128)(2,1)}, u32[]{:S(2)}) copy-start(bf16[1280,128]{1,0:T(8,128)(2,1)} %wk.1) | copy-start | bytes 983044
  29.5 1.7 copy-start.12
  29.6 2.5 %copy-start.2 = (bf16[1280,640]{1,0:T(8,128)(2,1)S(1)}, bf16[1280,640]{1,0:T(8,128)(2,1)}, u32[]{:S(2)}) copy-start(bf16[1280,640]{1,0:T(8,128)(2,1)} %wq.1) | copy-start | bytes 4915204
  32.1 1.4 copy-start.4
  34.0 2.2 %copy-start.6 = (bf16[1280,128]{1,0:T(8,128)(2,1)S(1)}, bf16[1280,128]{1,0:T(8,128)(2,1)}, u32[]{:S(2)}) copy-start(bf16[1280,128]{1,0:T(8,128)(2,1)} %wv.1) | copy-start | bytes 983044
  34.0 2.4 %copy-start.8 = (bf16[1280,128]{1,0:T(8,128)(2,1)S(1)}, bf16[1280,128]{1,0:T(8,128)(2,1)}, u32[]{:S(2)}) copy-start(bf16[1280,128]{1,0:T(8,128)(2,1)} %get-tuple-element.15) | copy-start | bytes 983044
  52.6 9.9 %copy-start.3 = (bf16[1280,640]{1,0:T(8,128)(2,1)S(1)}, bf16[1280,640]{1,0:T(8,128)(2,1)}, u32[]{:S(2)}) copy-start(bf16[1280,640]{1,0:T(8,128)(2,1)} %get-tuple-element.16) | copy-start | bytes 4915204
  61.3 1.8 copy-start.1
  63.8 11.1 %copy-start.7 = (bf16[1,128,640]{2,1,0:T(8,128)(2,1)S(1)}, bf16[1,128,640]{2,1,0:T(8,128)(2,1)}, u32[]{:S(2)}) copy-start(bf16[1,128,640]{2,1,0:T(8,128)(2,1)} %param.15) | copy-start | bytes 491524
  63.8 19.2 %copy-start.11 = (s32[1,128,6]{1,0,2:T(1,128)S(1)}, s32[1,128,6]{1,0,2:T(1,128)}, u32[]{:S(2)}) copy-start(s32[1,128,6]{1,0,2:T(1,128)} %param.25) | copy-start | bytes 9220
  86.0 119.0 %copy-start.10 = (f32[1,128,6]{1,0,2:T(1,128)S(1)}, f32[1,128,6]{1,0,2:T(1,128)}, u32[]{:S(2)}) copy-start(f32[1,128,6]{1,0,2:T(1,128)} %param.26) | copy-start | bytes 9220
  205.0 2.0 copy-start

commit v3 on v2

--- a/solution.py
+++ b/solution.py
@@ -178,30 +178,20 @@
     copies.finish()
 
 
-def suffix_kernel(own, kv, send, recv, sems):
-    local([(own, kv.at[0, 0])], sems)
-    greet([near("y", 1), near("y", -1), near("z", 1), near("z", -1)])
+def exchange_kernel(parts, got, send, recv, sems, transit):
+    me = lax.axis_index("head")
+    half = parts.shape[1] // 2
+    greet([near("x", 1), near("x", -1)])
     copies = Copies(send, recv)
-    torus_start(copies, kv, BACK, 0)
-    torus_run(copies, kv, BACK, 0)
-    copies.finish()
-
-
-def exchange_kernel(parts, got, send, recv, sems):
-    me = lax.axis_index("head")
-    greet([near("x", d) for d in range(1, X)])
-    copies = Copies(send, recv)
-    for d in (2, 1, 3):
-        to = lax.rem(me + d, X)
-        copies.start(d, parts.at[to], got.at[d - 1], near("x", d))
-    copies.finish()
-
-
-def small_kernel(block, got, send, recv, sems):
-    greet([near("x", d) for d in range(1, X)])
-    copies = Copies(send, recv)
-    for d in (2, 1, 3):
-        copies.start(d, block, got.at[d - 1], near("x", d))
+    right, left, opposite = (lax.rem(me + d, X) for d in (1, 3, 2))
+    copies.start("tr", parts.at[opposite, pl.ds(0, half)], transit.at[0], near("x", 1))
+    copies.start("tl", parts.at[opposite, pl.ds(half, half)], transit.at[1], near("x", -1))
+    copies.start("r", parts.at[right], got.at[0], near("x", 1))
+    copies.start("l", parts.at[left], got.at[2], near("x", -1))
+    copies.arrived("tr")
+    copies.start("rr", transit.at[0], got.at[1, pl.ds(0, half)], near("x", 1))
+    copies.arrived("tl")
+    copies.start("ll", transit.at[1], got.at[1, pl.ds(half, half)], near("x", -1))
     copies.finish()
 
 
@@ -228,8 +218,8 @@
 
 
 def experts_kernel(
-    outgoing, w_gate, w_up, w_down, back,
-    send, recv, sems, sent, came, sent_back, came_back, rows, hidden, results, wide, down,
+    outgoing, gain, w_gate, w_up, w_down, back,
+    send, recv, sems, sent, came, sent_back, came_back, rows, hidden, results, wide, down, normed,
 ):
     me = lax.axis_index("head")
     width = outgoing.shape[1]
@@ -295,7 +285,16 @@
         copies.arrived((("m", chunk), "rr"))
         copies.arrived((("m", chunk), "ll"))
         at = pl.ds(many * chunk, many)
-        both = jnp.dot(rows[at, :], wide[...], preferred_element_type=jnp.float32)
+        squares = jnp.zeros((many, 1), jnp.float32)
+        for part in range(X):
+            piece = rows[at, pl.ds(part * width, width)].astype(jnp.float32)
+            squares = squares + jnp.sum(piece * piece, axis=1, keepdims=True)
+        factor = lax.rsqrt(squares / (X * width) + NORM_EPS)
+        for part in range(X):
+            where = pl.ds(part * width, width)
+            piece = rows[at, where].astype(jnp.float32)
+            normed[:, where] = (piece * factor * gain[:, where].astype(jnp.float32)).astype(normed.dtype)
+        both = jnp.dot(normed[...], wide[...], preferred_element_type=jnp.float32)
         gate = both[:, :inner]
         hidden[at, own_hidden] = (gate / (1.0 + jnp.exp(-gate)) * both[:, inner:]).astype(hidden.dtype)
 
@@ -360,22 +359,21 @@
     return turned.astype(jnp.bfloat16)
 
 
-def attention_kernel(q, kv, sk, own_start, token_index, first, out):
+def attention_kernel(own, q, kv, own_start, token_index, first, out, send, recv, sems, sk):
     rows, dim = q.shape
     queries = q[...]
     scale = dim ** (-0.5)
-
-    def step(state, keys, values, visible):
+    copies_of_mask = rows // own_start.shape[0]
+
+    def step(state, keys, values, bias):
         top, total, summed = state
         scores = lax.dot_general(
             queries, keys, (((1,), (1,)), ((), ())), preferred_element_type=jnp.float32
         ) * scale
-        if visible is not None:
-            scores = jnp.where(visible, scores, MASKED)
+        if bias is not None:
+            scores = scores + bias
         new_top = jnp.maximum(top, jnp.max(scores, axis=1, keepdims=True))
         weights = jnp.exp(scores - new_top)
-        if visible is not None:
-            weights = jnp.where(visible, weights, 0.0)
         factor = jnp.exp(top - new_top)
         total = total * factor + jnp.sum(weights, axis=1, keepdims=True)
         summed = summed * factor + jnp.dot(
@@ -383,32 +381,51 @@
         )
         return new_top, total, summed
 
+    def prefix(index, state):
+        return step(state, kv[index, :, 0].reshape(-1, dim), kv[index, :, 1].reshape(-1, dim), None)
+
+    def suffix(index, state):
+        at = first[index, :][None, :]
+        visible = (at >= own_start[...]) & (at <= token_index[...])
+        bias = jnp.concatenate([jnp.where(visible, 0.0, MASKED)] * copies_of_mask, axis=0)
+        return step(state, sk[index, :, 0].reshape(-1, dim), sk[index, :, 1].reshape(-1, dim), bias)
+
+    local([(own, sk.at[0, 0])], sems)
+    greet([near("y", 1), near("y", -1), near("z", 1), near("z", -1)])
+    up, down, ahead = near("y", 1), near("y", -1), near("z", 1)
+    copies = Copies(send, recv)
+    torus_start(copies, sk, BACK, 0)
     state = (
         jnp.full((rows, 1), MASKED, jnp.float32),
         jnp.zeros((rows, 1), jnp.float32),
         jnp.zeros((rows, dim), jnp.float32),
     )
-
-    def prefix(index, state):
-        return step(
-            state,
-            kv[index, :, 0].reshape(-1, dim),
-            kv[index, :, 1].reshape(-1, dim),
-            None,
-        )
-
-    state = lax.fori_loop(0, kv.shape[0], prefix, state)
-
-    def suffix(index, state):
-        keys = sk[index, :, 0].reshape(-1, dim)
-        values = sk[index, :, 1].reshape(-1, dim)
-        at = first[index, :][None, :]
-        visible = (at >= own_start[...]) & (at <= token_index[...])
-        return step(state, keys, values, visible)
-
-    for index in range(sk.shape[0]):
-        state = suffix(index, state)
+    state = lax.fori_loop(0, Y // 2, prefix, state)
+    for slot in range(1, BACK + 1):
+        copies.arrived(("f", slot))
+        if slot < BACK:
+            copies.start(("f", slot + 1), sk.at[0, slot], sk.at[0, slot + 1], ahead)
+        copies.start(("u", slot), sk.at[0, slot], sk.at[1, slot], up)
+        copies.start(("d", slot), sk.at[0, slot], sk.at[3, slot], down)
+        if slot == 1:
+            copies.arrived(("u", 0))
+            copies.start(("v", 0), sk.at[1, 0], sk.at[2, 0], up)
+            state = lax.fori_loop(Y // 2, Y, prefix, state)
+    state = suffix(0, state)
+    copies.arrived(("u", 1))
+    copies.start(("v", 1), sk.at[1, 1], sk.at[2, 1], up)
+    copies.arrived(("d", 2))
+    copies.start(("v", 2), sk.at[3, 2], sk.at[2, 2], down)
+    copies.arrived(("u", 2))
+    state = suffix(1, state)
+    for slot in (0, 1):
+        copies.arrived(("d", slot))
+    state = suffix(3, state)
+    for slot in (0, 1, 2):
+        copies.arrived(("v", slot))
+    state = suffix(2, state)
     out[...] = (state[2] / state[1]).astype(out.dtype)
+    copies.finish()
 
 
 def on_device(
@@ -480,10 +497,6 @@
     suffix_own = jnp.stack(
         [apply_rotary(key_product, cosine, sine_part), value_product.astype(bf16)]
     )
-    suffix_kv = call(
-        suffix_kernel, 1, (suffix_own,), shape(Y, BACK + 1, 2, tok_dev, head_dim),
-        [VM], VM, torus_copies(BACK, 0),
-    )
     z_rank, y_rank = tok_rank // Y, tok_rank % Y
     y_from = (y_rank - jnp.arange(Y) + Y) % Y
     z_from = z_rank - jnp.arange(BACK + 1)
@@ -492,16 +505,12 @@
         device_from[:, :, None] * tok_dev + jnp.arange(tok_dev, dtype=jnp.int32)
     ).reshape(Y, (BACK + 1) * tok_dev)
     rows = group_length * tok_dev
-    attended = pl.pallas_call(
-        attention_kernel,
-        out_shape=shape(rows, head_dim),
-        in_specs=[VM] * 6,
-        out_specs=VM,
-    )(
-        queries, prefix_kv, suffix_kv,
-        jnp.tile(own_start[:, None], (group_length, 1)),
-        jnp.tile(token_index[:, None], (group_length, 1)),
-        key_index.astype(jnp.int32),
+    attended = call(
+        attention_kernel, 1,
+        (suffix_own, queries, prefix_kv, own_start[:, None], token_index[:, None],
+         key_index.astype(jnp.int32)),
+        shape(rows, head_dim), [VM] * 6, VM, torus_copies(BACK, 0),
+        (pltpu.VMEM((Y, BACK + 1, 2, tok_dev, head_dim), bf16),),
     )
     attended = jnp.transpose(attended.reshape(group_length, tok_dev, head_dim), (1, 0, 2)).reshape(
         tok_dev, group_length * head_dim
@@ -519,7 +528,8 @@
         [first_part[:, :share], first_part[:, share:], second_part[:, :share], second_part[:, share:]]
     )
     got = call(
-        exchange_kernel, 2, (parts,), shape(X - 1, tok_dev, share), [VM], VM, X - 1
+        exchange_kernel, 2, (parts,), shape(X - 1, tok_dev, share), [VM], VM, 6,
+        (pltpu.VMEM((2, tok_dev // 2, share), bf16),),
     )
     own_share = lax.dynamic_index_in_dim(parts, head_rank, 0, keepdims=False)
     mid = (
@@ -527,15 +537,6 @@
         + (own_share.astype(f32) + got[0].astype(f32) + got[1].astype(f32) + got[2].astype(f32))
     ).astype(bf16)
     mid_wide = mid.astype(f32)
-    squares = jnp.sum(mid_wide * mid_wide, axis=1)
-    small = jnp.broadcast_to(squares[None, :], (8, tok_dev))
-    small_got = call(
-        small_kernel, 3, (small,), shape(X - 1, 8, tok_dev, dtype=f32), [VM], VM, X - 1
-    )
-    mean_sq = (squares + small_got[0, 0] + small_got[1, 0] + small_got[2, 0]) / model_width
-    gain = lax.dynamic_slice_in_dim(moe_gain, head_rank * share, share, 0).astype(f32)
-    moe_in = (mid_wide * lax.rsqrt(mean_sq + NORM_EPS)[:, None] * gain).astype(bf16)
-
     experts = 2 * tok_count * w_gate.shape[0]
     top_count = expert_ids.shape[2]
     capacity = 4 * tok_dev * top_count // (3 * experts)
@@ -560,13 +561,13 @@
     spread_rank = jnp.dot(rank, spread, preferred_element_type=f32)
     placed = spread_rank == (slot_index % capacity).astype(f32)[None, :]
     outgoing = lax.dot_general(
-        placed.astype(bf16), moe_in, (((0,), (0,)), ((), ())), preferred_element_type=f32
+        placed.astype(bf16), mid, (((0,), (0,)), ((), ())), preferred_element_type=f32
     ).astype(bf16)
 
     inner = w_gate.shape[2]
     returned = call(
-        experts_kernel, 4, (outgoing, w_gate[0], w_up[0], w_down[0]), shape(slots, share),
-        [VM] + [HB] * 3, VM, 2 * 8 * 4,
+        experts_kernel, 4, (outgoing, moe_gain[None, :], w_gate[0], w_up[0], w_down[0]), shape(slots, share),
+        [VM] * 2 + [HB] * 3, VM, 2 * 8 * 4,
         (
             *[pltpu.SemaphoreType.DMA((64,))] * 4,
             pltpu.VMEM((slots, model_width), bf16),
@@ -574,6 +575,7 @@
             pltpu.VMEM((slots, share), bf16),
             pltpu.VMEM((model_width, 2 * inner), bf16),
             pltpu.VMEM((X * inner, share), bf16),
+            pltpu.VMEM((8 * capacity, model_width), bf16),
         ),
     )
 

time: 209 us -> 194 us (0.928)
  Pallas kernels: 183 us -> 170 us
    pallas_call x1 -> x0, Pallas kernels: 8.69 us -> none  [on_device(): pl.pallas_call(attention_kernel, out_shape=shape(rows, head_dim), in_spec...]
    pallas_call x5 -> x4, Pallas kernels: 175 us -> 170 us  [call(): pl.pallas_call(kernel, out_shape=outs, in_specs=in_specs, out_specs=out_s...]
where the time goes in v3:
time: 194 us; the launch traced here: 193 us
  Pallas kernels  170 us (88%)
  matrix products  10.5 us (5%)
  other arithmetic  8.59 us (4%)
  local copies, waits for them, and re-layouts  4.2 us (2%)
    pallas_call x4, Pallas kernels, call(): pl.pallas_call(kernel, out_shape=outs, in_specs=in_specs, out_specs=out_s...  170 us

profile of v3, /device:TPU:1, one launch (start us, length us, event | category | flops | bytes accessed | tf_op | source)
XLA Modules:
  0.0 193.2 jit_solution(2012060709963551802)
XLA Ops:
  0.0 26.8 %shard_map.145 = (bf16[128,2560]{1,0:T(8,128)(2,1)}, bf16[4,8,2,64,128]{4,3,2,1,0:T(8,128)(2,1)}, bf16[1280,640]{1,0:T(8,128)(2,1)}, bf16[1280,128]{1,0:T(8,128)...) custom-call(bf16[128,640]{1,0:T(8,128)(2,1)} %bitcast.91, bf16[64,128]{1,0:T(8,128)(2,1)} %bitcast.95, ...), custom_call_target="tpu_custom_call" | custom-call | tf_op jit(solution)/shard_map/pallas_call | solution.py:139
  26.8 0.0 copy-start.5
  26.8 1.3 fusion
  28.2 0.0 copy-done.8
  28.2 1.3 fusion.2
  29.5 0.0 copy-start.12
  29.6 0.0 copy-start.2
  29.6 0.2 fusion.71
  29.9 1.4 convolution_add_fusion.3
  31.3 0.2 reduce-window_clone.1
  31.5 0.1 select_reduce_fusion.1
  31.6 0.3 multiply_cosine_fusion
  31.9 0.1 copy.36
  32.0 0.1 copy.37
  32.1 0.0 copy-done.2
  32.1 0.4 fusion.73
  32.5 1.0 copy-done.4
  33.5 0.4 convolution_add_fusion.1
  33.9 0.0 copy-start.6
  34.0 0.2 copy.35
  34.1 0.1 subtract_convert_fusion
  34.2 0.2 copy.38
  34.3 0.2 copy.39
  34.5 0.8 pad_maximum_fusion.1.q
  35.3 0.2 fusion.72
  35.6 1.3 fusion.10
  36.9 0.7 pad_maximum_fusion.2.own
  37.6 0.1 select_multiply_fusion
  37.7 0.7 bitcast_add_fusion.1.first
  38.4 0.7 copy.40.own_start
  39.1 0.6 iota_add_fusion.token_index
  39.8 15.5 %shard_map.146 = bf16[640,128]{1,0:T(8,128)(2,1)} custom-call(bf16[2,128,128]{2,1,0:T(8,128)(2,1)} %pad_maximum_fusion.2.own, bf16[640,128]{1,0:T(8,128)(2,1)} %pad_maximum_fusion.1.q, bf16[4,8,2,64,128]{4,3,2,1,0:T(8,128)(2,1)} %get-tuple-element.15.kv, s32[128,1]{1,0:T(8,128)} %copy.40.own_start, s32[128,1]{1,0:T(8,128)} %iota_add_fusion.token_index, ...), custom_call_target="tpu_custom_call" | custom-call | tf_op jit(solution)/shard_map/pallas_call | solution.py:139
  55.3 1.1 copy.41
  56.4 0.6 convolution_convert_fusion
  57.0 0.6 broadcast_select_fusion.1
  57.6 0.0 copy-start.7
  57.6 0.1 slice_bitcast_fusion.1
  57.7 0.0 copy-start.11
  57.7 0.9 pad_maximum_fusion.parts
  58.6 9.1 %shard_map.147 = bf16[3,128,640]{2,1,0:T(8,128)(2,1)} custom-call(bf16[4,128,640]{2,1,0:T(8,128)(2,1)} %pad_maximum_fusion.parts), custom_call_target="tpu_custom_call" | custom-call | tf_op jit(solution)/shard_map/pallas_call | solution.py:139
  67.8 0.0 copy-start.9
  67.8 1.3 fusion.12
  69.2 0.5 convolution_compare_fusion
  69.7 1.6 convolution_convert_fusion.2.outgoing
  71.3 0.6 broadcast_in_dim.89.gain
  71.9 118.0 %shard_map.148 = bf16[1024,640]{1,0:T(8,128)(2,1)} custom-call(bf16[1024,640]{1,0:T(8,128)(2,1)} %convolution_convert_fusion.2.outgoing, bf16[1,2560]{1,0:T(2,128)(2,1)} %broadcast_in_dim.89.gain, bf16[2560,384]{1,0:T(8,128)(2,1)} %bitcast.85, bf16[2560,384]{1,0:T(8,128)(2,1)} %bitcast.86, bf16[1536,640]{1,0:T(8,128)(2,1)} %bitcast.87), custom_call_target="tpu_custom_call" | custom-call | tf_op jit(solution)/shard_map/pallas_call | solution.py:139
  190.0 1.9 %fusion.6 = f32[128,640]{1,0:T(8,128)S(1)} fusion(bf16[1024,640]{1,0:T(8,128)(2,1)} %shard_map.148, pred[128,1024]{1,0:T(32,128)(4,1)S(1)} %convolution_compare_fusion, s32[1024]{0:T(1024)S(1)} %get-tuple-element.33, f32[128,64]{0,1:T(8,128)S(1)} %select_reduce_fusion), kind=kOutput, calls=%fused_computation.16 | convolution fusion | flops 184885248 | bytes 1806336 | tf_op jit(solution)/shard_map/dot_general | solution.py:584
  192.0 1.2 fusion.8
  (33 shorter events, 0.2 us)
Async XLA Ops:
  0.0 28.2 %copy-start.8 = (bf16[2560]{0:T(1024)(128)(2,1)S(1)}, bf16[2560]{0:T(1024)(128)(2,1)}, u32[]{:S(2)}) copy-start(bf16[2560]{0:T(1024)(128)(2,1)} %param.16) | copy-start | bytes 15364
  26.8 2.8 %copy-start.5 = (bf16[1280,128]{1,0:T(8,128)(2,1)S(1)}, bf16[1280,128]{1,0:T(8,128)(2,1)}, u32[]{:S(2)}) copy-start(bf16[1280,128]{1,0:T(8,128)(2,1)} %wk.1) | copy-start | bytes 983044
  29.5 1.7 copy-start.12
  29.6 2.5 %copy-start.2 = (bf16[1280,640]{1,0:T(8,128)(2,1)S(1)}, bf16[1280,640]{1,0:T(8,128)(2,1)}, u32[]{:S(2)}) copy-start(bf16[1280,640]{1,0:T(8,128)(2,1)} %wq.1) | copy-start | bytes 4915204
  32.1 1.4 copy-start.4
  33.9 1.4 copy-start.6
  35.6 20.8 %copy-start.3 = (bf16[1280,640]{1,0:T(8,128)(2,1)S(1)}, bf16[1280,640]{1,0:T(8,128)(2,1)}, u32[]{:S(2)}) copy-start(bf16[1280,640]{1,0:T(8,128)(2,1)} %get-tuple-element.16) | copy-start | bytes 4915204
  39.8 17.2 %copy-start.1 = (bf16[1280,640]{1,0:T(8,128)(2,1)S(1)}, bf16[1280,640]{1,0:T(8,128)(2,1)}, u32[]{:S(2)}) copy-start(bf16[1280,640]{1,0:T(8,128)(2,1)} %wo.1) | copy-start | bytes 4915204
  57.6 10.2 %copy-start.7 = (bf16[1,128,640]{2,1,0:T(8,128)(2,1)S(1)}, bf16[1,128,640]{2,1,0:T(8,128)(2,1)}, u32[]{:S(2)}) copy-start(bf16[1,128,640]{2,1,0:T(8,128)(2,1)} %param.15) | copy-start | bytes 491524
  57.7 11.4 %copy-start.11 = (s32[1,128,6]{1,0,2:T(1,128)S(1)}, s32[1,128,6]{1,0,2:T(1,128)}, u32[]{:S(2)}) copy-start(s32[1,128,6]{1,0,2:T(1,128)} %param.25) | copy-start | bytes 9220
  67.8 3.5 %copy-start.9 = (bf16[2560]{0:T(1024)(128)(2,1)S(1)}, bf16[2560]{0:T(1024)(128)(2,1)}, u32[]{:S(2)}) copy-start(bf16[2560]{0:T(1024)(128)(2,1)} %param.24) | copy-start | bytes 15364
  71.9 118.1 %copy-start.10 = (f32[1,128,6]{1,0,2:T(1,128)S(1)}, f32[1,128,6]{1,0,2:T(1,128)}, u32[]{:S(2)}) copy-start(f32[1,128,6]{1,0,2:T(1,128)} %param.26) | copy-start | bytes 9220
  190.0 2.0 %copy-start = (bf16[1024,640]{1,0:T(8,128)(2,1)S(1)}, bf16[1024,640]{1,0:T(8,128)(2,1)}, u32[]{:S(2)}) copy-start(bf16[1024,640]{1,0:T(8,128)(2,1)} %shard_map.148) | copy-start | bytes 3932164

commit v4 on v3

--- a/solution.py
+++ b/solution.py
@@ -73,29 +73,35 @@
     copies.start(("d", 0), kv.at[0, 0], kv.at[3, 0], down)
 
 
-def torus_run(copies, kv, forward, backward):
+def torus_step(copies, kv, forward, backward, step):
     up, down = near("y", 1), near("y", -1)
     last = forward + backward
-    for step in range(1, max(forward, backward) + 1):
-        for mark, reach, slot, following, way in (
-            ("f", forward, step, step + 1, 1),
-            ("b", backward, last + 1 - step, last - step, -1),
-        ):
-            if step > reach:
-                continue
-            copies.arrived((mark, step))
-            if step < reach:
-                copies.start((mark, step + 1), kv.at[0, slot], kv.at[0, following], near("z", way))
-            copies.start(("u", slot), kv.at[0, slot], kv.at[1, slot], up)
-            copies.start(("d", slot), kv.at[0, slot], kv.at[3, slot], down)
-    half = (last + 1) // 2
-    for slot in range(last + 1):
-        if slot <= half:
+    for mark, reach, slot, following, way in (
+        ("f", forward, step, step + 1, 1),
+        ("b", backward, last + 1 - step, last - step, -1),
+    ):
+        if step > reach:
+            continue
+        copies.arrived((mark, step))
+        if step < reach:
+            copies.start((mark, step + 1), kv.at[0, slot], kv.at[0, following], near("z", way))
+        copies.start(("u", slot), kv.at[0, slot], kv.at[1, slot], up)
+        copies.start(("d", slot), kv.at[0, slot], kv.at[3, slot], down)
+
+
+def torus_cross(copies, kv, last, *slots):
+    for slot in slots:
+        if slot <= (last + 1) // 2:
             copies.arrived(("u", slot))
-            copies.start(("v", slot), kv.at[1, slot], kv.at[2, slot], up)
+            copies.start(("v", slot), kv.at[1, slot], kv.at[2, slot], near("y", 1))
         else:
             copies.arrived(("d", slot))
-            copies.start(("v", slot), kv.at[3, slot], kv.at[2, slot], down)
+            copies.start(("v", slot), kv.at[3, slot], kv.at[2, slot], near("y", -1))
+
+
+def column(copies, mark):
+    for key in [key for key in copies.open if key[0] == mark]:
+        copies.arrived(key)
 
 
 def torus_copies(forward, backward):
@@ -144,7 +150,7 @@
         scratch_shapes=[
             pltpu.SemaphoreType.DMA((copies,)),
             pltpu.SemaphoreType.DMA((copies,)),
-            pltpu.SemaphoreType.DMA((4,)),
+            pltpu.SemaphoreType.DMA((6,)),
             *extra,
         ],
         compiler_params=pltpu.CompilerParams(collective_id=ident, has_side_effects=True),
@@ -155,9 +161,26 @@
     return jax.ShapeDtypeStruct(dims, dtype)
 
 
-def prologue_kernel(hid, pk, pv, wq, wk, wv, wo, feat, kv, wq2, wk2, wv2, wo2, send, recv, sems):
-    me = lax.axis_index("head")
-    width = hid.shape[1]
+def front_kernel(
+    hid, gain, pk, pv, wq, wk, wv, wo, cosine, sine, own_start, token_index, first, out, wo2,
+    send, recv, sems, send2, recv2, feat, normed, kv, sk, wide, queries,
+):
+    me, grp = lax.axis_index("head"), lax.axis_index("grp")
+    tokens, width = hid.shape
+    depth, across = wq.shape
+    dim = pk.shape[1]
+    heads = across // dim
+    rows = heads * tokens
+    scale = dim ** (-0.5)
+    mine = pl.ds(pl.multiple_of(grp * depth, depth), depth)
+    places = [
+        (wq, wide.at[mine, pl.ds(0, across)]),
+        (wk, wide.at[mine, pl.ds(across, dim)]),
+        (wv, wide.at[mine, pl.ds(across + dim, dim)]),
+    ]
+    own_weights = [pltpu.make_async_copy(a, b, sems.at[3 + i]) for i, (a, b) in enumerate(places)]
+    for copy in own_weights:
+        copy.start()
     local(
         [
             (pk, kv.at[0, 0, 0]),
@@ -170,12 +193,101 @@
     greet([near("x", 1), near("x", -1), near("y", 1), near("y", -1), near("z", 1), near("z", -1), core])
     copies = Copies(send, recv)
     torus_start(copies, kv, 4, 3)
-    ring_start(copies, "h", feat, width, hid.shape[0], 0)
-    for key, a, b in (("q", wq, wq2), ("k", wk, wk2), ("w", wv, wv2), ("o", wo, wo2)):
+    ring_start(copies, "h", feat, width, tokens, 0)
+    for key, (a, b) in zip(("wq", "wk", "wv"), places):
         copies.start(key, a, b, core)
-    torus_run(copies, kv, 4, 3)
-    ring_relay(copies, "h", feat, width, hid.shape[0], 0)
+    copies.start("wo", wo, wo2, core)
+    torus_step(copies, kv, 4, 3, 1)
+    ring_relay(copies, "h", feat, width, tokens, 0)
+    torus_step(copies, kv, 4, 3, 2)
+    torus_cross(copies, kv, 7, 0, 1, 7)
+    torus_step(copies, kv, 4, 3, 3)
+
+    copies.arrived(("h", "rr"))
+    copies.arrived(("h", "ll"))
+    for copy in own_weights:
+        copy.wait()
+    for key in ("wq", "wk", "wv"):
+        copies.arrived(key)
+    squares = jnp.zeros((tokens, 1), jnp.float32)
+    for part in range(X):
+        piece = feat[:, pl.ds(part * width, width)].astype(jnp.float32)
+        squares = squares + jnp.sum(piece * piece, axis=1, keepdims=True)
+    factor = lax.rsqrt(squares / (X * width) + NORM_EPS)
+    for part in range(X):
+        where = pl.ds(part * width, width)
+        piece = feat[:, where].astype(jnp.float32)
+        normed[:, where] = (piece * factor * gain[:, where].astype(jnp.float32)).astype(normed.dtype)
+    product = jnp.dot(normed[...], wide[...], preferred_element_type=jnp.float32)
+
+    def turned(head):
+        part = product[:, head * dim : (head + 1) * dim]
+        return (part * cosine[...] + pltpu.roll(part, dim // 2, 1) * sine[...]).astype(jnp.bfloat16)
+
+    sk[0, 0, 0] = turned(heads)
+    sk[0, 0, 1] = product[:, across + dim :].astype(jnp.bfloat16)
+    for head in range(heads):
+        queries[pl.ds(head * tokens, tokens), :] = turned(head)
+
+    torus_step(copies, kv, 4, 3, 4)
+    torus_cross(copies, kv, 7, 2, 6)
+    later = Copies(send2, recv2)
+    torus_start(later, sk, BACK, 0)
+
+    def step(state, keys, values, bias):
+        top, total, summed = state
+        scores = lax.dot_general(
+            queries[...], keys, (((1,), (1,)), ((), ())), preferred_element_type=jnp.float32
+        ) * scale
+        if bias is not None:
+            scores = scores + bias
+        new_top = jnp.maximum(top, jnp.max(scores, axis=1, keepdims=True))
+        weights = jnp.exp(scores - new_top)
+        shrink = jnp.exp(top - new_top)
+        total = total * shrink + jnp.sum(weights, axis=1, keepdims=True)
+        summed = summed * shrink + jnp.dot(
+            weights.astype(jnp.bfloat16), values, preferred_element_type=jnp.float32
+        )
+        return new_top, total, summed
+
+    def prefix(index, state):
+        return step(state, kv[index, :, 0].reshape(-1, dim), kv[index, :, 1].reshape(-1, dim), None)
+
+    def suffix(index, state):
+        at = first[index, :][None, :]
+        visible = (at >= own_start[...]) & (at <= token_index[...])
+        bias = jnp.concatenate([jnp.where(visible, 0.0, MASKED)] * heads, axis=0)
+        return step(state, sk[index, :, 0].reshape(-1, dim), sk[index, :, 1].reshape(-1, dim), bias)
+
+    state = (
+        jnp.full((rows, 1), MASKED, jnp.float32),
+        jnp.zeros((rows, 1), jnp.float32),
+        jnp.zeros((rows, dim), jnp.float32),
+    )
+    state = prefix(0, state)
+    torus_cross(copies, kv, 7, 3, 5, 4)
+    torus_step(later, sk, BACK, 0, 1)
+    column(copies, "u")
+    state = prefix(1, state)
+    torus_step(later, sk, BACK, 0, 2)
+    torus_cross(later, sk, BACK, 0)
+    column(copies, "d")
+    state = prefix(3, state)
+    torus_cross(later, sk, BACK, 1, 2)
+    column(copies, "v")
+    state = prefix(2, state)
+    state = suffix(0, state)
+    column(later, "u")
+    state = suffix(1, state)
+    column(later, "d")
+    state = suffix(3, state)
+    column(later, "v")
+    _, total, summed = suffix(2, state)
+    result = summed / total
+    for head in range(heads):
+        out[:, head * dim : (head + 1) * dim] = result[head * tokens : (head + 1) * tokens].astype(out.dtype)
     copies.finish()
+    later.finish()
 
 
 def exchange_kernel(parts, got, send, recv, sems, transit):
@@ -328,14 +440,6 @@
     each(1, 64, lambda slot: home(slot).wait())
 
 
-def rms_norm(values_in, gain_vector):
-    widened = values_in.astype(jnp.float32)
-    mean_sq = jnp.mean(widened * widened, axis=-1, keepdims=True)
-    return (widened * lax.rsqrt(mean_sq + NORM_EPS) * gain_vector.astype(jnp.float32)).astype(
-        jnp.bfloat16
-    )
-
-
 def rotary_tables(token_positions, head_dim):
     half_dim = head_dim // 2
     frequency = jnp.exp(
@@ -343,89 +447,6 @@
     )
     angles = token_positions.astype(jnp.float32)[:, None] * frequency[None, :]
     return jnp.cos(angles), jnp.sin(angles)
-
-
-def apply_rotary(product, cosine, sine_part):
-    half_dim = product.shape[-1] // 2
-    first_half = product[..., :half_dim]
-    second_half = product[..., half_dim:]
-    turned = jnp.concatenate(
-        [
-            first_half * cosine - second_half * sine_part,
-            second_half * cosine + first_half * sine_part,
-        ],
-        axis=-1,
-    )
-    return turned.astype(jnp.bfloat16)
-
-
-def attention_kernel(own, q, kv, own_start, token_index, first, out, send, recv, sems, sk):
-    rows, dim = q.shape
-    queries = q[...]
-    scale = dim ** (-0.5)
-    copies_of_mask = rows // own_start.shape[0]
-
-    def step(state, keys, values, bias):
-        top, total, summed = state
-        scores = lax.dot_general(
-            queries, keys, (((1,), (1,)), ((), ())), preferred_element_type=jnp.float32
-        ) * scale
-        if bias is not None:
-            scores = scores + bias
-        new_top = jnp.maximum(top, jnp.max(scores, axis=1, keepdims=True))
-        weights = jnp.exp(scores - new_top)
-        factor = jnp.exp(top - new_top)
-        total = total * factor + jnp.sum(weights, axis=1, keepdims=True)
-        summed = summed * factor + jnp.dot(
-            weights.astype(jnp.bfloat16), values, preferred_element_type=jnp.float32
-        )
-        return new_top, total, summed
-
-    def prefix(index, state):
-        return step(state, kv[index, :, 0].reshape(-1, dim), kv[index, :, 1].reshape(-1, dim), None)
-
-    def suffix(index, state):
-        at = first[index, :][None, :]
-        visible = (at >= own_start[...]) & (at <= token_index[...])
-        bias = jnp.concatenate([jnp.where(visible, 0.0, MASKED)] * copies_of_mask, axis=0)
-        return step(state, sk[index, :, 0].reshape(-1, dim), sk[index, :, 1].reshape(-1, dim), bias)
-
-    local([(own, sk.at[0, 0])], sems)
-    greet([near("y", 1), near("y", -1), near("z", 1), near("z", -1)])
-    up, down, ahead = near("y", 1), near("y", -1), near("z", 1)
-    copies = Copies(send, recv)
-    torus_start(copies, sk, BACK, 0)
-    state = (
-        jnp.full((rows, 1), MASKED, jnp.float32),
-        jnp.zeros((rows, 1), jnp.float32),
-        jnp.zeros((rows, dim), jnp.float32),
-    )
-    state = lax.fori_loop(0, Y // 2, prefix, state)
-    for slot in range(1, BACK + 1):
-        copies.arrived(("f", slot))
-        if slot < BACK:
-            copies.start(("f", slot + 1), sk.at[0, slot], sk.at[0, slot + 1], ahead)
-        copies.start(("u", slot), sk.at[0, slot], sk.at[1, slot], up)
-        copies.start(("d", slot), sk.at[0, slot], sk.at[3, slot], down)
-        if slot == 1:
-            copies.arrived(("u", 0))
-            copies.start(("v", 0), sk.at[1, 0], sk.at[2, 0], up)
-            state = lax.fori_loop(Y // 2, Y, prefix, state)
-    state = suffix(0, state)
-    copies.arrived(("u", 1))
-    copies.start(("v", 1), sk.at[1, 1], sk.at[2, 1], up)
-    copies.arrived(("d", 2))
-    copies.start(("v", 2), sk.at[3, 2], sk.at[2, 2], down)
-    copies.arrived(("u", 2))
-    state = suffix(1, state)
-    for slot in (0, 1):
-        copies.arrived(("d", slot))
-    state = suffix(3, state)
-    for slot in (0, 1, 2):
-        copies.arrived(("v", slot))
-    state = suffix(2, state)
-    out[...] = (state[2] / state[1]).astype(out.dtype)
-    copies.finish()
 
 
 def on_device(
@@ -458,15 +479,6 @@
     share = model_width // X
     quarter = hidden_in[0]
 
-    features, prefix_kv, other_query, other_key, other_value, other_out = call(
-        prologue_kernel, 0,
-        (quarter, prefix_keys[0, :, 0], cached_prefix_values[0, :, 0], w_query,
-         key_projection_weight, value_projection_weight, w_out),
-        (shape(tok_dev, model_width), shape(Y, Z, 2, prefix_dev, head_dim), shape(*w_query.shape),
-         shape(*key_projection_weight.shape), shape(*value_projection_weight.shape), shape(*w_out.shape)),
-        [VM] * 3 + [HB] * 4, [VM] * 2 + [HB] * 4, torus_copies(4, 3) + 8,
-    )
-    attention_input = rms_norm(features, attn_gain)
     lengths = request_lengths[0]
     request_ends = jnp.cumsum(lengths)
     starts = request_ends - lengths
@@ -477,26 +489,6 @@
     token_positions = prefix_dev * tok_count + token_index - own_start
     cosine, sine_part = rotary_tables(token_positions, head_dim)
 
-    half = model_width // 2
-    lower = attention_input[:, :half]
-    upper = attention_input[:, half:]
-    mine = jnp.where(grp_rank == 0, lower, upper)
-    others = jnp.where(grp_rank == 0, upper, lower)
-
-    def project(own, other):
-        return jnp.dot(mine, own, preferred_element_type=f32) + jnp.dot(
-            others, other, preferred_element_type=f32
-        )
-
-    query_product = project(w_query, other_query).reshape(tok_dev, group_length, head_dim)
-    key_product = project(key_projection_weight, other_key)
-    value_product = project(value_projection_weight, other_value)
-    queries = apply_rotary(
-        jnp.transpose(query_product, (1, 0, 2)), cosine[None], sine_part[None]
-    ).reshape(group_length * tok_dev, head_dim)
-    suffix_own = jnp.stack(
-        [apply_rotary(key_product, cosine, sine_part), value_product.astype(bf16)]
-    )
     z_rank, y_rank = tok_rank // Y, tok_rank % Y
     y_from = (y_rank - jnp.arange(Y) + Y) % Y
     z_from = z_rank - jnp.arange(BACK + 1)
@@ -504,16 +496,23 @@
     key_index = (
         device_from[:, :, None] * tok_dev + jnp.arange(tok_dev, dtype=jnp.int32)
     ).reshape(Y, (BACK + 1) * tok_dev)
-    rows = group_length * tok_dev
-    attended = call(
-        attention_kernel, 1,
-        (suffix_own, queries, prefix_kv, own_start[:, None], token_index[:, None],
-         key_index.astype(jnp.int32)),
-        shape(rows, head_dim), [VM] * 6, VM, torus_copies(BACK, 0),
-        (pltpu.VMEM((Y, BACK + 1, 2, tok_dev, head_dim), bf16),),
-    )
-    attended = jnp.transpose(attended.reshape(group_length, tok_dev, head_dim), (1, 0, 2)).reshape(
-        tok_dev, group_length * head_dim
+    attended, other_out = call(
+        front_kernel, 0,
+        (quarter, attn_gain[None, :], prefix_keys[0, :, 0], cached_prefix_values[0, :, 0], w_query,
+         key_projection_weight, value_projection_weight, w_out,
+         jnp.concatenate([cosine, cosine], axis=1), jnp.concatenate([-sine_part, sine_part], axis=1),
+         own_start[:, None], token_index[:, None], key_index.astype(jnp.int32)),
+        (shape(tok_dev, group_length * head_dim), shape(*w_out.shape)),
+        [VM] * 4 + [HB] * 4 + [VM] * 5, [VM, HB], torus_copies(4, 3) + 8,
+        (
+            *[pltpu.SemaphoreType.DMA((torus_copies(BACK, 0),))] * 2,
+            pltpu.VMEM((tok_dev, model_width), bf16),
+            pltpu.VMEM((tok_dev, model_width), bf16),
+            pltpu.VMEM((Y, Z, 2, prefix_dev, head_dim), bf16),
+            pltpu.VMEM((Y, BACK + 1, 2, tok_dev, head_dim), bf16),
+            pltpu.VMEM((model_width, (group_length + 2) * head_dim), bf16),
+            pltpu.VMEM((group_length * tok_dev, head_dim), bf16),
+        ),
     )
 
     def out_part(weights):

time: 194 us -> 175 us (0.902)
  Pallas kernels: 170 us -> 157 us
  matrix products: 10.5 us -> 8.06 us
  other arithmetic: 8.59 us -> 6.36 us
    pallas_call x4 -> x3, Pallas kernels: 170 us -> 157 us  [call(): pl.pallas_call(kernel, out_shape=outs, in_specs=in_specs, out_specs=out_s...]
    dot_general x6 -> x0, matrix products: 4 us -> none  [the longest x3 3.12 us: project(): jnp.dot(others, other, preferred_element_type=f32)]
where the time goes in v4:
time: 175 us
  Pallas kernels  157 us (90%)
  matrix products  8.06 us (5%)
  other arithmetic  6.36 us (4%)
  local copies, waits for them, and re-layouts  2.74 us (2%)
    pallas_call x3, Pallas kernels, call(): pl.pallas_call(kernel, out_shape=outs, in_specs=in_specs, out_specs=out_s...  157 us

profile of v4, /device:TPU:1, one launch (start us, length us, event | category | flops | bytes accessed | tf_op | source)
XLA Modules:
  0.0 174.8 jit_solution(13809966323340583234)
XLA Ops:
  0.0 0.1 select_multiply_fusion
  0.1 0.7 bitcast_add_fusion.1.first
  0.8 0.8 reduce-window_clone.1
  1.6 0.7 subtract_bitcast_fusion
  2.3 0.1 select_reduce_fusion.1
  2.4 0.3 fusion.21
  2.7 0.7 pad_maximum_fusion.1
  3.5 0.7 copy.22.own_start
  4.2 0.6 iota_add_fusion.token_index
  4.8 1.3 broadcast_in_dim.78.gain
  6.1 33.5 %shard_map.145 = (bf16[128,640]{1,0:T(8,128)(2,1)}, bf16[1280,640]{1,0:T(8,128)(2,1)}) custom-call(bf16[128,640]{1,0:T(8,128)(2,1)} %bitcast.61, bf16[1,2560]{1,0:T(2,128)(2,1)} %broadcast_in_dim.78.gain, bf16[64,128]{1,0:T(8,128)(2,1)} %bitcast.62, bf16[64,128]{1,0:T(8,128)(2,1)} %bitcast.63, bf16[1280,640]{1,0:T(8,128)(2,1)} %wq.1, bf16[1280,128]{1,0:T(8,128)(2,1)} %wk.1, ...), custom_call_target="tpu_custom_call" | custom-call | tf_op jit(solution)/shard_map/pallas_call | solution.py:145
  39.6 0.0 copy-start.1
  39.6 0.0 copy-start.2
  39.6 2.2 %convolution_convert_fusion = bf16[128,1280]{1,0:T(8,128)(2,1)S(1)} fusion(bf16[128,640]{1,0:T(8,128)(2,1)} %get-tuple-element.7, bf16[1280,640]{1,0:T(8,128)(2,1)} %get-tuple-element.8), kind=kOutput, calls=%fused_computation | convolution fusion | flops 209879040 | bytes 2129920 | tf_op jit(solution)/shard_map/dot_general | solution.py:519
  41.9 0.0 copy-done.1
  41.9 0.0 copy-done.2
  41.9 0.6 broadcast_select_fusion.1
  42.5 0.0 copy-start.3
  42.6 0.0 copy-start.6
  42.6 0.9 pad_maximum_fusion.parts
  43.5 9.2 %shard_map.146 = bf16[3,128,640]{2,1,0:T(8,128)(2,1)} custom-call(bf16[4,128,640]{2,1,0:T(8,128)(2,1)} %pad_maximum_fusion.parts), custom_call_target="tpu_custom_call" | custom-call | tf_op jit(solution)/shard_map/pallas_call | solution.py:145
  52.7 0.0 copy-done.3
  52.7 0.0 copy-start.4
  52.7 1.3 fusion.7
  54.0 0.0 copy-done.6
  54.1 0.5 convolution_compare_fusion
  54.6 1.6 convolution_convert_fusion.2.outgoing
  56.2 0.0 copy-done.4
  56.2 0.6 broadcast_in_dim.89.gain
  56.8 0.0 copy-start.5
  56.8 114.7 %shard_map.147 = bf16[1024,640]{1,0:T(8,128)(2,1)} custom-call(bf16[1024,640]{1,0:T(8,128)(2,1)} %convolution_convert_fusion.2.outgoing, bf16[1,2560]{1,0:T(2,128)(2,1)} %broadcast_in_dim.89.gain, bf16[2560,384]{1,0:T(8,128)(2,1)} %bitcast.58, bf16[2560,384]{1,0:T(8,128)(2,1)} %bitcast.59, bf16[1536,640]{1,0:T(8,128)(2,1)} %bitcast.60), custom_call_target="tpu_custom_call" | custom-call | tf_op jit(solution)/shard_map/pallas_call | solution.py:145
  171.6 0.0 copy-done.5
  171.6 0.0 copy-start
  171.6 1.9 %fusion.3 = f32[128,640]{1,0:T(8,128)S(1)} fusion(bf16[1024,640]{1,0:T(8,128)(2,1)} %shard_map.147, pred[128,1024]{1,0:T(32,128)(4,1)S(1)} %convolution_compare_fusion, s32[1024]{0:T(1024)S(1)} %get-tuple-element.18, f32[128,64]{0,1:T(8,128)S(1)} %select_reduce_fusion), kind=kOutput, calls=%fused_computation.10 | convolution fusion | flops 184885248 | bytes 1806336 | tf_op jit(solution)/shard_map/dot_general | solution.py:583
  173.6 0.0 copy-done
  173.6 1.2 fusion.5
  (15 shorter events, 0.2 us)
Async XLA Ops:
  39.6 2.3 %copy-start.1 = (bf16[1280,640]{1,0:T(8,128)(2,1)S(1)}, bf16[1280,640]{1,0:T(8,128)(2,1)}, u32[]{:S(2)}) copy-start(bf16[1280,640]{1,0:T(8,128)(2,1)} %wo.1) | copy-start | bytes 4915204
  39.6 2.3 %copy-start.2 = (bf16[128,640]{1,0:T(8,128)(2,1)S(1)}, bf16[128,640]{1,0:T(8,128)(2,1)}, u32[]{:S(2)}) copy-start(bf16[128,640]{1,0:T(8,128)(2,1)} %get-tuple-element.7) | copy-start | bytes 491524
  42.5 10.2 %copy-start.3 = (bf16[1,128,640]{2,1,0:T(8,128)(2,1)S(1)}, bf16[1,128,640]{2,1,0:T(8,128)(2,1)}, u32[]{:S(2)}) copy-start(bf16[1,128,640]{2,1,0:T(8,128)(2,1)} %param.15) | copy-start | bytes 491524
  42.6 11.4 %copy-start.6 = (s32[1,128,6]{1,0,2:T(1,128)S(1)}, s32[1,128,6]{1,0,2:T(1,128)}, u32[]{:S(2)}) copy-start(s32[1,128,6]{1,0,2:T(1,128)} %param.25) | copy-start | bytes 9220
  52.7 3.5 %copy-start.4 = (bf16[2560]{0:T(1024)(128)(2,1)S(1)}, bf16[2560]{0:T(1024)(128)(2,1)}, u32[]{:S(2)}) copy-start(bf16[2560]{0:T(1024)(128)(2,1)} %param.24) | copy-start | bytes 15364
  56.8 114.7 %copy-start.5 = (f32[1,128,6]{1,0,2:T(1,128)S(1)}, f32[1,128,6]{1,0,2:T(1,128)}, u32[]{:S(2)}) copy-start(f32[1,128,6]{1,0,2:T(1,128)} %param.26) | copy-start | bytes 9220
  171.6 2.0 %copy-start = (bf16[1024,640]{1,0:T(8,128)(2,1)S(1)}, bf16[1024,640]{1,0:T(8,128)(2,1)}, u32[]{:S(2)}) copy-start(bf16[1024,640]{1,0:T(8,128)(2,1)} %shard_map.147) | copy-start | bytes 3932164

commit v5 on v4

--- a/solution.py
+++ b/solution.py
@@ -290,23 +290,6 @@
     later.finish()
 
 
-def exchange_kernel(parts, got, send, recv, sems, transit):
-    me = lax.axis_index("head")
-    half = parts.shape[1] // 2
-    greet([near("x", 1), near("x", -1)])
-    copies = Copies(send, recv)
-    right, left, opposite = (lax.rem(me + d, X) for d in (1, 3, 2))
-    copies.start("tr", parts.at[opposite, pl.ds(0, half)], transit.at[0], near("x", 1))
-    copies.start("tl", parts.at[opposite, pl.ds(half, half)], transit.at[1], near("x", -1))
-    copies.start("r", parts.at[right], got.at[0], near("x", 1))
-    copies.start("l", parts.at[left], got.at[2], near("x", -1))
-    copies.arrived("tr")
-    copies.start("rr", transit.at[0], got.at[1, pl.ds(0, half)], near("x", 1))
-    copies.arrived("tl")
-    copies.start("ll", transit.at[1], got.at[1, pl.ds(half, half)], near("x", -1))
-    copies.finish()
-
-
 def partner(slot, sign):
     tok = lax.axis_index("tok")
     grp = lax.axis_index("grp")
@@ -316,7 +299,7 @@
     return {"grp": lax.rem(grp + dg, 2), "tok": z * Y + y}
 
 
-def greet_all(more):
+def signal_all(more):
     barrier = pltpu.get_barrier_semaphore()
 
     def body(slot, carry):
@@ -326,16 +309,18 @@
     lax.fori_loop(1, 64, body, 0)
     for device in more:
         pl.semaphore_signal(barrier, inc=1, device_id=device, device_id_type=MESH)
-    pl.semaphore_wait(barrier, 63 + len(more))
+    return barrier, 63 + len(more)
 
 
 def experts_kernel(
-    outgoing, gain, w_gate, w_up, w_down, back,
-    send, recv, sems, sent, came, sent_back, came_back, rows, hidden, results, wide, down, normed,
+    attended, hid, placed, gain, w_out, other_out, w_gate, w_up, w_down, back, mid,
+    send, recv, sems, sent, came, sent_back, came_back, sent_part, came_part,
+    outgoing, rows, hidden, results, wide, down, normed, wide_out, parts, got, transit,
 ):
+    grp = lax.axis_index("grp")
     me = lax.axis_index("head")
-    width = outgoing.shape[1]
-    cap = outgoing.shape[0] // 64
+    width = hid.shape[1]
+    cap = placed.shape[0] // 64
     inner = w_gate.shape[1]
     many = 8 * cap
     columns = pl.ds(pl.multiple_of(me * width, 128), width)
@@ -374,12 +359,49 @@
         pltpu.make_async_copy(w_down, down, sems.at[2]),
     ]
     own = pltpu.make_async_copy(outgoing.at[block(0), :], rows.at[block(0), columns], sems.at[3])
-    own.start()
-    for copy in weights:
+    half_out = w_out.shape[0]
+    projections = [
+        pltpu.make_async_copy(w_out, wide_out.at[0], sems.at[4]),
+        pltpu.make_async_copy(other_out, wide_out.at[1], sems.at[5]),
+    ]
+    barrier, greetings = signal_all([near("x", 1), near("x", -1)])
+    for copy in projections + weights:
         copy.start()
-    greet_all([near("x", 1), near("x", -1)])
+    for copy in projections:
+        copy.wait()
+    for side in range(2):
+        for part in range(half_out // width):
+            parts[2 * lax.rem(grp + side, 2) + part] = lax.dot_general(
+                attended[...], wide_out[side, pl.ds(part * width, width), :],
+                (((1,), (1,)), ((), ())), preferred_element_type=jnp.float32,
+            ).astype(parts.dtype)
+    pl.semaphore_wait(barrier, greetings)
+
+    shares = Copies(sent_part, came_part)
+    middle = parts.shape[1] // 2
+    right, left, opposite = (lax.rem(me + d, X) for d in (1, 3, 2))
+    upper, lower = pl.ds(0, middle), pl.ds(middle, middle)
+    shares.start("tr", parts.at[opposite, upper], transit.at[0], near("x", 1))
+    shares.start("tl", parts.at[opposite, lower], transit.at[1], near("x", -1))
+    shares.start("r", parts.at[right], got.at[0], near("x", 1))
+    shares.start("l", parts.at[left], got.at[2], near("x", -1))
+    shares.arrived("tr")
+    shares.start("rr", transit.at[0], got.at[1, upper], near("x", 1))
+    shares.arrived("tl")
+    shares.start("ll", transit.at[1], got.at[1, lower], near("x", -1))
+    for key in ("r", "l", "rr", "ll"):
+        shares.arrived(key)
+    total = parts[me].astype(jnp.float32)
+    for index in range(X - 1):
+        total = total + got[index].astype(jnp.float32)
+    mid[...] = (hid[...].astype(jnp.float32) + total).astype(mid.dtype)
+    outgoing[...] = jnp.dot(
+        placed[...], mid[...], preferred_element_type=jnp.float32
+    ).astype(outgoing.dtype)
+    shares.finish()
     for chunk in CHUNK_ORDER:
         of_chunk(chunk, lambda slot: there(slot).start())
+    own.start()
     own.wait()
     for copy in weights:
         copy.wait()
@@ -469,7 +491,6 @@
     f32, bf16 = jnp.float32, jnp.bfloat16
     tok_count = lax.axis_size("tok")
     tok_rank = lax.axis_index("tok")
-    head_rank = lax.axis_index("head")
     grp_rank = lax.axis_index("grp")
     tok_dev = hidden_in.shape[1]
     model_width = attn_gain.shape[0]
@@ -515,27 +536,6 @@
         ),
     )
 
-    def out_part(weights):
-        return lax.dot_general(
-            attended, weights, (((1,), (1,)), ((), ())), preferred_element_type=f32
-        ).astype(bf16)
-
-    own_part, other_part = out_part(w_out), out_part(other_out)
-    first_part = jnp.where(grp_rank == 0, own_part, other_part)
-    second_part = jnp.where(grp_rank == 0, other_part, own_part)
-    parts = jnp.stack(
-        [first_part[:, :share], first_part[:, share:], second_part[:, :share], second_part[:, share:]]
-    )
-    got = call(
-        exchange_kernel, 2, (parts,), shape(X - 1, tok_dev, share), [VM], VM, 6,
-        (pltpu.VMEM((2, tok_dev // 2, share), bf16),),
-    )
-    own_share = lax.dynamic_index_in_dim(parts, head_rank, 0, keepdims=False)
-    mid = (
-        quarter.astype(f32)
-        + (own_share.astype(f32) + got[0].astype(f32) + got[1].astype(f32) + got[2].astype(f32))
-    ).astype(bf16)
-    mid_wide = mid.astype(f32)
     experts = 2 * tok_count * w_gate.shape[0]
     top_count = expert_ids.shape[2]
     capacity = 4 * tok_dev * top_count // (3 * experts)
@@ -559,22 +559,31 @@
     spread = (slot_index[None, :] // capacity == jnp.arange(experts, dtype=jnp.int32)[:, None]).astype(bf16)
     spread_rank = jnp.dot(rank, spread, preferred_element_type=f32)
     placed = spread_rank == (slot_index % capacity).astype(f32)[None, :]
-    outgoing = lax.dot_general(
-        placed.astype(bf16), mid, (((0,), (0,)), ((), ())), preferred_element_type=f32
-    ).astype(bf16)
+    spread_rows = lax.dot_general(
+        spread, rank, (((0,), (1,)), ((), ())), preferred_element_type=f32
+    )
+    placed_rows = (spread_rows == (slot_index % capacity).astype(f32)[:, None]).astype(bf16)
 
     inner = w_gate.shape[2]
-    returned = call(
-        experts_kernel, 4, (outgoing, moe_gain[None, :], w_gate[0], w_up[0], w_down[0]), shape(slots, share),
-        [VM] * 2 + [HB] * 3, VM, 2 * 8 * 4,
+    returned, mid = call(
+        experts_kernel, 4,
+        (attended, quarter, placed_rows, moe_gain[None, :], w_out, other_out, w_gate[0], w_up[0], w_down[0]),
+        (shape(slots, share), shape(tok_dev, share)),
+        [VM] * 4 + [HB] * 5, [VM] * 2, 2 * 8 * 4,
         (
             *[pltpu.SemaphoreType.DMA((64,))] * 4,
+            *[pltpu.SemaphoreType.DMA((6,))] * 2,
+            pltpu.VMEM((slots, share), bf16),
             pltpu.VMEM((slots, model_width), bf16),
             pltpu.VMEM((slots, X * inner), bf16),
             pltpu.VMEM((slots, share), bf16),
             pltpu.VMEM((model_width, 2 * inner), bf16),
             pltpu.VMEM((X * inner, share), bf16),
             pltpu.VMEM((8 * capacity, model_width), bf16),
+            pltpu.VMEM((2, *w_out.shape), bf16),
+            pltpu.VMEM((X, tok_dev, share), bf16),
+            pltpu.VMEM((X - 1, tok_dev, share), bf16),
+            pltpu.VMEM((2, tok_dev // 2, share), bf16),
         ),
     )
 
@@ -582,7 +591,7 @@
         spread_weight = jnp.where(placed, jnp.dot(part, spread, preferred_element_type=f32), 0.0)
         return jnp.dot(spread_weight.astype(bf16), returned, preferred_element_type=f32)
 
-    output = (mid_wide + (combine(weight_hi) + combine(weight_lo))).astype(bf16)
+    output = (mid.astype(f32) + (combine(weight_hi) + combine(weight_lo))).astype(bf16)
     return output[None]
 
 

time: 175 us -> 169 us (0.966)
  matrix products: 8.06 us -> 4.7 us
  other arithmetic: 6.36 us -> 4.16 us
    dot_general x3 -> x2, matrix products: 4.44 us -> 1.31 us  [the longest x1 1.11 us: on_device(): lax.dot_general(spread, rank, (((0,), (1,)), ((), ())), preferred_element...]
    pallas_call x3 -> x2, Pallas kernels: 157 us -> 157 us  [call(): pl.pallas_call(kernel, out_shape=outs, in_specs=in_specs, out_specs=out_s...]
where the time goes in v5:
time: 169 us
  Pallas kernels  157 us (93%)
  matrix products  4.7 us (3%)
  other arithmetic  4.16 us (2%)
  local copies, waits for them, and re-layouts  2.65 us (2%)
    pallas_call x2, Pallas kernels, call(): pl.pallas_call(kernel, out_shape=outs, in_specs=in_specs, out_specs=out_s...  157 us

profile of v5, /device:TPU:1, one launch (start us, length us, event | category | flops | bytes accessed | tf_op | source)
XLA Modules:
  0.0 168.5 jit_solution(6797026701902696719)
XLA Ops:
  0.1 0.1 select_multiply_fusion
  0.1 0.7 bitcast_add_fusion.first
  0.8 0.8 reduce-window_clone.1
  1.6 0.7 subtract_bitcast_fusion
  2.3 0.1 select_reduce_fusion.1
  2.4 0.3 fusion.20
  2.7 0.7 pad_maximum_fusion
  3.5 0.7 copy.22.own_start
  4.2 0.6 iota_add_fusion.token_index
  4.8 1.3 broadcast_in_dim.79.gain
  6.1 0.0 copy-start.4
  6.1 0.0 copy-start.2
  6.1 33.5 %shard_map.145 = (bf16[128,640]{1,0:T(8,128)(2,1)}, bf16[1280,640]{1,0:T(8,128)(2,1)}) custom-call(bf16[128,640]{1,0:T(8,128)(2,1)} %bitcast.44, bf16[1,2560]{1,0:T(2,128)(2,1)} %broadcast_in_dim.79.gain, bf16[64,128]{1,0:T(8,128)(2,1)} %bitcast.46, bf16[64,128]{1,0:T(8,128)(2,1)} %bitcast.47, bf16[1280,640]{1,0:T(8,128)(2,1)} %wq.1, bf16[1280,128]{1,0:T(8,128)(2,1)} %wk.1, ...), custom_call_target="tpu_custom_call" | custom-call | tf_op jit(solution)/shard_map/pallas_call | solution.py:145
  39.6 0.0 copy-done.4
  39.7 0.2 fusion.7
  39.9 1.1 fusion.5.placed
  41.0 0.0 copy-done.2
  41.0 0.6 broadcast_in_dim.86.gain
  41.6 0.0 copy-start.3
  41.6 123.4 %shard_map.146 = (bf16[1024,640]{1,0:T(8,128)(2,1)}, bf16[128,640]{1,0:T(8,128)(2,1)}) custom-call(bf16[128,640]{1,0:T(8,128)(2,1)} %get-tuple-element.9.attended, bf16[128,640]{1,0:T(8,128)(2,1)} %bitcast.45, bf16[1024,128]{1,0:T(8,128)(2,1)} %fusion.5.placed, bf16[1,2560]{1,0:T(2,128)(2,1)} %broadcast_in_dim.86.gain, bf16[1280,640]{1,0:T(8,128)(2,1)} %w_out.1, ...), custom_call_target="tpu_custom_call" | custom-call | tf_op jit(solution)/shard_map/pallas_call | solution.py:145
  165.0 0.0 copy-start
  165.0 0.0 copy-start.1
  165.1 0.3 convolution_compare_fusion
  165.3 0.0 copy-done.3
  165.4 1.9 %fusion.3 = f32[128,640]{1,0:T(8,128)S(1)} fusion(bf16[1024,640]{1,0:T(8,128)(2,1)} %get-tuple-element.12, pred[128,1024]{1,0:T(32,128)(4,1)S(1)} %convolution_compare_fusion, s32[1024]{0:T(1024)S(1)} %get-tuple-element.18, f32[128,64]{0,1:T(8,128)S(1)} %select_reduce_fusion), kind=kOutput, calls=%fused_computation.8 | convolution fusion | flops 184885248 | bytes 1806336 | tf_op jit(solution)/shard_map/dot_general | solution.py:592
  167.3 0.0 copy-done
  167.3 0.0 copy-done.1
  167.3 1.2 fusion.6
  (13 shorter events, 0.1 us)
Async XLA Ops:
  6.1 33.5 %copy-start.4 = (s32[1,128,6]{1,0,2:T(1,128)S(1)}, s32[1,128,6]{1,0,2:T(1,128)}, u32[]{:S(2)}) copy-start(s32[1,128,6]{1,0,2:T(1,128)} %param.25) | copy-start | bytes 9220
  6.1 34.9 %copy-start.2 = (bf16[2560]{0:T(1024)(128)(2,1)S(1)}, bf16[2560]{0:T(1024)(128)(2,1)}, u32[]{:S(2)}) copy-start(bf16[2560]{0:T(1024)(128)(2,1)} %param.24) | copy-start | bytes 15364
  41.6 123.7 %copy-start.3 = (f32[1,128,6]{1,0,2:T(1,128)S(1)}, f32[1,128,6]{1,0,2:T(1,128)}, u32[]{:S(2)}) copy-start(f32[1,128,6]{1,0,2:T(1,128)} %param.26) | copy-start | bytes 9220
  165.0 2.3 %copy-start = (bf16[1024,640]{1,0:T(8,128)(2,1)S(1)}, bf16[1024,640]{1,0:T(8,128)(2,1)}, u32[]{:S(2)}) copy-start(bf16[1024,640]{1,0:T(8,128)(2,1)} %get-tuple-element.12) | copy-start | bytes 3932164
  165.0 2.3 %copy-start.1 = (bf16[128,640]{1,0:T(8,128)(2,1)S(1)}, bf16[128,640]{1,0:T(8,128)(2,1)}, u32[]{:S(2)}) copy-start(bf16[128,640]{1,0:T(8,128)(2,1)} %get-tuple-element.11) | copy-start | bytes 491524

commit v6 on v5

--- a/solution.py
+++ b/solution.py
@@ -399,8 +399,14 @@
         placed[...], mid[...], preferred_element_type=jnp.float32
     ).astype(outgoing.dtype)
     shares.finish()
-    for chunk in CHUNK_ORDER:
-        of_chunk(chunk, lambda slot: there(slot).start())
+    there(8 * CHUNK_ORDER[1]).start()
+    for one, two in zip(CHUNK_ORDER[0::2], CHUNK_ORDER[1::2]):
+        def both_ways(index, carry):
+            there(8 * one + index).start()
+            there(8 * two + index).start()
+            return carry
+
+        lax.fori_loop(0 if one else 1, 8, both_ways, 0)
     own.start()
     own.wait()
     for copy in weights:

time: 169 us -> 167 us (0.988)
  Pallas kernels: 157 us -> 155 us
    pallas_call x2, Pallas kernels: 157 us -> 155 us  [call(): pl.pallas_call(kernel, out_shape=outs, in_specs=in_specs, out_specs=out_s...]
where the time goes in v6:
time: 167 us
  Pallas kernels  155 us (93%)
  matrix products  4.7 us (3%)
  other arithmetic  4.16 us (2%)
  local copies, waits for them, and re-layouts  2.65 us (2%)
    pallas_call x2, Pallas kernels, call(): pl.pallas_call(kernel, out_shape=outs, in_specs=in_specs, out_specs=out_s...  155 us

profile of v6, /device:TPU:1, one launch (start us, length us, event | category | flops | bytes accessed | tf_op | source)
XLA Modules:
  0.0 166.7 jit_solution(8139087145524521939)
XLA Ops:
  0.1 0.1 select_multiply_fusion
  0.1 0.7 bitcast_add_fusion.first
  0.8 0.8 reduce-window_clone.1
  1.6 0.7 subtract_bitcast_fusion
  2.3 0.1 select_reduce_fusion.1
  2.4 0.3 fusion.20
  2.7 0.7 pad_maximum_fusion
  3.5 0.7 copy.22.own_start
  4.2 0.6 iota_add_fusion.token_index
  4.8 1.3 broadcast_in_dim.79.gain
  6.1 0.0 copy-start.4
  6.1 0.0 copy-start.2
  6.1 33.5 %shard_map.145 = (bf16[128,640]{1,0:T(8,128)(2,1)}, bf16[1280,640]{1,0:T(8,128)(2,1)}) custom-call(bf16[128,640]{1,0:T(8,128)(2,1)} %bitcast.44, bf16[1,2560]{1,0:T(2,128)(2,1)} %broadcast_in_dim.79.gain, bf16[64,128]{1,0:T(8,128)(2,1)} %bitcast.46, bf16[64,128]{1,0:T(8,128)(2,1)} %bitcast.47, bf16[1280,640]{1,0:T(8,128)(2,1)} %wq.1, bf16[1280,128]{1,0:T(8,128)(2,1)} %wk.1, ...), custom_call_target="tpu_custom_call" | custom-call | tf_op jit(solution)/shard_map/pallas_call | solution.py:145
  39.6 0.0 copy-done.4
  39.7 0.2 fusion.7
  39.9 1.1 fusion.5.placed
  41.0 0.0 copy-done.2
  41.0 0.6 broadcast_in_dim.86.gain
  41.6 0.0 copy-start.3
  41.6 121.6 %shard_map.146 = (bf16[1024,640]{1,0:T(8,128)(2,1)}, bf16[128,640]{1,0:T(8,128)(2,1)}) custom-call(bf16[128,640]{1,0:T(8,128)(2,1)} %get-tuple-element.9.attended, bf16[128,640]{1,0:T(8,128)(2,1)} %bitcast.45, bf16[1024,128]{1,0:T(8,128)(2,1)} %fusion.5.placed, bf16[1,2560]{1,0:T(2,128)(2,1)} %broadcast_in_dim.86.gain, bf16[1280,640]{1,0:T(8,128)(2,1)} %w_out.1, ...), custom_call_target="tpu_custom_call" | custom-call | tf_op jit(solution)/shard_map/pallas_call | solution.py:145
  163.2 0.0 copy-start
  163.2 0.0 copy-start.1
  163.2 0.3 convolution_compare_fusion
  163.5 0.0 copy-done.3
  163.6 1.9 %fusion.3 = f32[128,640]{1,0:T(8,128)S(1)} fusion(bf16[1024,640]{1,0:T(8,128)(2,1)} %get-tuple-element.12, pred[128,1024]{1,0:T(32,128)(4,1)S(1)} %convolution_compare_fusion, s32[1024]{0:T(1024)S(1)} %get-tuple-element.18, f32[128,64]{0,1:T(8,128)S(1)} %select_reduce_fusion), kind=kOutput, calls=%fused_computation.8 | convolution fusion | flops 184885248 | bytes 1806336 | tf_op jit(solution)/shard_map/dot_general | solution.py:598
  165.5 0.0 copy-done
  165.5 0.0 copy-done.1
  165.5 1.2 fusion.6
  (13 shorter events, 0.1 us)
Async XLA Ops:
  6.1 33.5 %copy-start.4 = (s32[1,128,6]{1,0,2:T(1,128)S(1)}, s32[1,128,6]{1,0,2:T(1,128)}, u32[]{:S(2)}) copy-start(s32[1,128,6]{1,0,2:T(1,128)} %param.25) | copy-start | bytes 9220
  6.1 34.9 %copy-start.2 = (bf16[2560]{0:T(1024)(128)(2,1)S(1)}, bf16[2560]{0:T(1024)(128)(2,1)}, u32[]{:S(2)}) copy-start(bf16[2560]{0:T(1024)(128)(2,1)} %param.24) | copy-start | bytes 15364
  41.6 121.9 %copy-start.3 = (f32[1,128,6]{1,0,2:T(1,128)S(1)}, f32[1,128,6]{1,0,2:T(1,128)}, u32[]{:S(2)}) copy-start(f32[1,128,6]{1,0,2:T(1,128)} %param.26) | copy-start | bytes 9220
  163.2 2.3 %copy-start = (bf16[1024,640]{1,0:T(8,128)(2,1)S(1)}, bf16[1024,640]{1,0:T(8,128)(2,1)}, u32[]{:S(2)}) copy-start(bf16[1024,640]{1,0:T(8,128)(2,1)} %get-tuple-element.12) | copy-start | bytes 3932164
  163.2 2.3 %copy-start.1 = (bf16[128,640]{1,0:T(8,128)(2,1)S(1)}, bf16[128,640]{1,0:T(8,128)(2,1)}, u32[]{:S(2)}) copy-start(bf16[128,640]{1,0:T(8,128)(2,1)} %get-tuple-element.11) | copy-start | bytes 491524
